TPU v7x, 256 devices: a whole 4x4x8 slice. The times are simulated.
256 devices in a mesh: aux: 64 (over y, z, core), blk: 4 (over x).
Axes of the slice: x: 4, y: 4, z: 8, core: 2. Of those that a mesh axis runs over, the one named last changes fastest.
Arguments:
- half_blocks: bfloat16 [32768, 64, 512], P(('aux', 'blk')), may hold values from -0.0625 to 0.0625
- screen: int32 [2048, 64], P(('aux', 'blk')), may hold values from 0 to 1, as said below
- domain_length: int32 [64], P('aux'), may hold values from 128 to 512, as said below
- domain_index: int32 [64, 512], P('aux'), may hold values from 0 to 19999, as said below
- orbital_coeff: bfloat16 [20000, 64], replicated, may hold values from -6 to 6
Outputs:
- exchange_block: float32 [64, 512, 512], P('aux', 'blk')
- exchange_orbital: float32 [64, 64, 512], P('aux', None, 'blk')
Inputs may be any that keep to these rules, and one draw needn't show every extreme that they name: `screen`: within every aligned run of 8 tiles each orbital keeps at least 2 and at most 4 tiles; one orbital keeps exactly 4 in every run. `domain_length`: some orbital's domain is full. `domain_index`: each orbital's row holds distinct basis functions in increasing order.
All inputs are finite; a program needn't handle non-finite values.
Results may differ from a plain program's by a relative error of at most 0.00045.
Values may be sent and summed in bfloat16 or wider, within the bound.
No kernel may reach another device: no remote copies, remote signals or barrier semaphores. Data moves between devices by JAX's collectives and lax.ppermute only.
A program may use at most 64 MiB of HBM per device.

v0:
```python
import jax
import jax.numpy as jnp
from jax import lax
from jax.sharding import PartitionSpec as P


def split_up(value, dim, devices):
    before, after = (value.shape[:dim], value.shape[dim + 1 :])
    return jnp.moveaxis(value.reshape(*before, devices, -1, *after), dim, 0)


def summed_on_arrival(value, axis, dim):
    tiles = split_up(value, dim, lax.axis_size(axis))
    arrived = lax.all_to_all(tiles, axis, split_axis=0, concat_axis=0, tiled=True)
    return arrived.sum(axis=0)


def per_device(half_blocks, screen, domain_length, domain_index, orbital_coeff):
    slab_rows, orbitals, dom_width = half_blocks.shape
    tile_count = screen.shape[0]
    tiled = half_blocks.reshape(tile_count, slab_rows // tile_count, orbitals, dom_width)
    keep_count = tile_count // 2
    position = lax.broadcasted_iota(jnp.int32, screen.shape, 0)
    ranking = (1 - screen) * tile_count + position
    chosen = jnp.argsort(ranking, axis=0)[:keep_count]
    kept_flags = jnp.take_along_axis(screen, chosen, axis=0).astype(jnp.bfloat16)
    picked = jnp.zeros((keep_count,) + tiled.shape[1:], jnp.bfloat16)
    for tile_slot in range(tile_count):
        picked = jnp.where((chosen == tile_slot)[:, None, :, None], tiled[tile_slot][None], picked)
    picked = picked * kept_flags[:, None, :, None]
    packed = picked.reshape(keep_count * tiled.shape[1], orbitals, dom_width)
    arrived = lax.all_to_all(packed, "aux", split_axis=1, concat_axis=0, tiled=True)
    columns = arrived[:, 0, :]
    row_share = dom_width // lax.axis_size("blk")
    gram_part = summed_on_arrival(
        lax.dot_general(
            columns, columns, (((0,), (0,)), ((), ())), preferred_element_type=jnp.float32
        ),
        "blk",
        0,
    )
    length = domain_length[0]
    row_place = lax.axis_index("blk") * row_share + lax.iota(jnp.int32, row_share)
    col_place = lax.iota(jnp.int32, dom_width)
    inside = ((row_place < length)[:, None] & (col_place < length)[None, :]).astype(jnp.float32)
    exch_rows = gram_part * inside
    local_coeff = jnp.take(orbital_coeff, domain_index[0], axis=0).astype(jnp.float32)
    occ_rows = jnp.einsum("ab,bj->ja", exch_rows, local_coeff, precision=lax.Precision.HIGHEST)
    return (exch_rows[None], occ_rows[None])


def solution(mesh):
    return jax.shard_map(
        per_device,
        mesh=mesh,
        in_specs=(
            P(("aux", "blk"), None, None),
            P(("aux", "blk"), None),
            P("aux"),
            P("aux", None),
            P(),
        ),
        out_specs=(P("aux", "blk", None), P("aux", None, "blk")),
        check_vma=False,
    )
```

profile of v0, /device:TPU:3, one launch (start us, length us, event | category | flops | bytes accessed | tf_op | source)
XLA Modules:
  0.0 167.2 jit_solution(8395134111381926016)
XLA Ops:
  0.6 0.7 iota_add_fusion
  1.3 0.7 sort.17
  2.1 0.1 copy.19
  2.2 0.1 copy.21
  2.9 3.9 %fusion.18 = (bf16[16,64,512]{2,1,0:T(8,128)(2,1)S(1)}, bf16[16,64,512]{2,1,0:T(8,128)(2,1)S(1)}, bf16[16,64,512]{2,1,0:T(8,128)(2,1)S(1)}, bf16[16,64,512]{2,1,...) fusion(bf16[128,64,512]{2,1,0:T(8,128)(2,1)} %param.5), kind=kLoop, calls=%fused_computation.41 | loop fusion | bytes 16777216 | tf_op jit(solution)/shard_map/slice | solution.py:29
  6.9 0.6 copy.18
  7.4 0.6 copy.20
  8.0 0.6 copy.22
  8.6 1.6 copy.24
  10.2 1.6 copy.26
  11.7 1.6 copy.28
  13.3 1.6 copy.30
  14.9 1.6 copy.32
  16.6 1.4 gather_fusion.1
  18.2 7.8 %fusion.7 = bf16[64,64,512]{2,0,1:T(8,128)(2,1)S(1)} fusion(pred[64,64]{0,1:T(8,128)(4,1)S(1)} %copy.31, pred[64,64]{0,1:T(8,128)(4,1)S(1)} %copy.29, pred[64,64]{0,1:T(8,128)(4,1)S(1)} %copy.27, pred[64,64]{0,1:T(8,128)(4,1)S(1)} %copy.25, pred[64,64]{0,1:T(8,128)(4,1)S(1)} %copy.23, pred[64,64]{0,1:T(8,128)(4,1)S(1)} %copy.21, ...), kind=kLoop, calls=%fused_computation.10 | loop fusion | flops 18874368 | bytes 12623872 | tf_op jit(solution)/shard_map/mul | solution.py:30
  26.0 108.4 %all_to_all.20 = bf16[64,64,512]{2,0,1:T(8,128)(2,1)} all-to-all(bf16[64,64,512]{2,0,1:T(8,128)(2,1)S(1)} %fusion.7), channel_id=1, replica_groups=mesh['aux'=64,'blk'=4] {'aux'}, dimensions={1} | all-to-all | bytes 8388608 | tf_op jit(solution)/shard_map/all_to_all | solution.py:32
  134.4 6.5 %copy.36 = bf16[512,4096]{1,0:T(8,128)(2,1)} copy(bf16[512,4096]{0,1:T(8,128)(2,1)} %bitcast.68) | data formatting | bytes 8388608 | tf_op jit(solution)/shard_map/dot_general | solution.py:36
  140.8 6.9 %fusion.19 = f32[4,128,512]{2,1,0:T(8,128)} fusion(bf16[4,128,4096]{2,1,0:T(8,128)(2,1)} %bitcast.70, bf16[4096,512,1]{1,0,2:T(8,128)(2,1)} %bitcast.69), kind=kOutput, calls=%fused_computation.42 | convolution fusion | flops 2147483648 | bytes 9437184 | tf_op jit(solution)/shard_map/dot_general | solution.py:36
  147.7 4.3 %all-to-all-start.1 = ((f32[4,128,512]{2,1,0:T(8,128)}), f32[4,128,512]{2,1,0:T(8,128)S(1)}, u32[]{:S(2)}, u32[]{:S(2)}) async-start(f32[4,128,512]{2,1,0:T(8,128)} %fusion.19), calls=%async_computation.1 | async-start | bytes 2097152 | tf_op jit(solution)/shard_map/all_to_all | solution.py:14
  152.6 5.9 %copy.35 = bf16[20000,64]{1,0:T(8,128)(2,1)} copy(bf16[20000,64]{0,1:T(8,128)(2,1)} %param.9) | data formatting | bytes 5120000 | tf_op args[4]
  158.5 4.2 %gather_fusion = bf16[512,64]{1,0:T(8,128)(2,1)S(1)} fusion(bf16[20000,64]{1,0:T(8,128)(2,1)} %copy.35, s32[1024]{0:T(1024)S(1)} %pad_clamp_fusion), kind=kCustom, calls=%fused_computation | custom fusion | bytes 133120 | tf_op jit(solution)/shard_map/jit(_take)/gather | solution.py:47
  162.7 2.6 %all-to-all-done.1 = f32[4,128,512]{2,1,0:T(8,128)S(1)} async-done(((f32[4,128,512]{2,1,0:T(8,128)}), f32[4,128,512]{2,1,0:T(8,128)S(1)}, u32[]{:S(2)}, u32[]{:S(2)}) %all-to-all-start.1) | async-done | bytes 1048608 | tf_op jit(solution)/shard_map/all_to_all | solution.py:14
  165.4 0.8 bitcast_select_fusion.1
  166.2 1.1 convolution_bitcast_fusion
  (31 shorter events, 1.0 us)
Async XLA Ops:
  10.2 6.4 %copy-start = (s32[8,64]{1,0:T(8,128)S(1)}, s32[8,64]{1,0:T(8,128)}, u32[]{:S(2)}) copy-start(s32[8,64]{1,0:T(8,128)} %param.6) | copy-start | bytes 6148
  147.7 17.6 %all-to-all-start.1 = ((f32[4,128,512]{2,1,0:T(8,128)}), f32[4,128,512]{2,1,0:T(8,128)S(1)}, u32[]{:S(2)}, u32[]{:S(2)}) async-start(f32[4,128,512]{2,1,0:T(8,128)} %fusion.19), calls=%async_computation.1 | async-start | bytes 2097152 | tf_op jit(solution)/shard_map/all_to_all | solution.py:14
  151.9 6.5 %copy-start.1 = (s32[1,512]{1,0:T(1,128)S(1)}, s32[1,512]{1,0:T(1,128)}, u32[]{:S(2)}) copy-start(s32[1,512]{1,0:T(1,128)} %param.8) | copy-start | bytes 6148
where the time goes:
time: 170 us; the launch traced here: 167 us
  blocking collectives  108 us (64%)
  local copies, waits for them, and re-layouts  32.5 us (19%)
  other arithmetic  10.1 us (6%)
  matrix products  7.93 us (5%)
  starting transfers between devices  4.26 us (3%)
  waiting for transfers between devices  2.59 us (2%)
    all_to_all x1, blocking collectives, per_device(): lax.all_to_all(packed, 'aux', split_axis=1, concat_axis=0, tiled=True)  108 us
    slice x9, local copies, waits for them, and re-layouts, per_device(): tiled[tile_slot][None]  13.5 us
    mul x1, other arithmetic, per_device(): picked = picked * kept_flags[:, None, :, None]  7.79 us
    dot_general x1, matrix products, per_device(): lax.dot_general(columns, columns, (((0,), (0,)), ((), ())), preferred_ele...  6.86 us
    dot_general x1, local copies, waits for them, and re-layouts, per_device(): lax.dot_general(columns, columns, (((0,), (0,)), ((), ())), preferred_ele...  6.45 us
    unnamed x5, local copies, waits for them, and re-layouts  5.86 us
    all_to_all x1, starting transfers between devices, summed_on_arrival(): lax.all_to_all(tiles, axis, split_axis=0, concat_axis=0, tiled=True)  4.26 us
    gather x1, local copies, waits for them, and re-layouts, per_device(): jnp.take(orbital_coeff, domain_index[0], axis=0).astype(jnp.float32)  4.16 us
  transfers between devices with their start and end apart: 1, of which 1 were waited for; matrix products, arithmetic and copies ran while one was open for 6% of the time, Pallas kernels for 0%

commit v1 on v0

v1 whole, which is shorter than its diff:
```python
import jax
import jax.numpy as jnp
from jax import lax
from jax.experimental import pallas as pl
from jax.experimental.pallas import tpu as pltpu
from jax.sharding import Mesh
from jax.sharding import PartitionSpec as P

TILES = 8
SLOTS = 4
TROWS = 16
HALF = 8
OG = 8
SHARES = 4
NONE = -1000


def pack_kernel(code_ref, x_ref, o_ref, pick_ref):
    step = pl.program_id(0)
    width = TILES * HALF * OG
    place = lax.broadcasted_iota(jnp.int32, (HALF, width), 1) - OG * lax.broadcasted_iota(
        jnp.int32, (HALF, width), 0
    )
    for i in range(OG):
        for k in range(0, SLOTS, 2):
            pair = [
                jnp.where(place == code_ref[k + d, step * OG + i], 1.0, 0.0) for d in range(2)
            ]
            row = (i * SLOTS + k) * HALF
            pick_ref[row : row + 2 * HALF, :] = jnp.concatenate(pair, axis=0).astype(jnp.bfloat16)
    for h in range(2):
        rows = x_ref[:, h].astype(jnp.float32).reshape(width, x_ref.shape[-1]).astype(jnp.bfloat16)
        got = jnp.dot(pick_ref[...], rows, preferred_element_type=jnp.float32)
        got = got.astype(jnp.bfloat16).reshape(OG, SLOTS * HALF, x_ref.shape[-1])
        o_ref[:, h * SLOTS * HALF : (h + 1) * SLOTS * HALF, :] = got


def pack(code, half_blocks):
    rows, orbitals, width = half_blocks.shape
    tiled = half_blocks.reshape(TILES, 2, HALF, orbitals, width)
    kept = rows // TILES * SLOTS
    return pl.pallas_call(
        pack_kernel,
        grid_spec=pltpu.PrefetchScalarGridSpec(
            num_scalar_prefetch=1,
            grid=(orbitals // OG,),
            in_specs=[pl.BlockSpec((TILES, 2, HALF, OG, width), lambda s, c: (0, 0, 0, s, 0))],
            out_specs=pl.BlockSpec((OG, kept, width), lambda s, c: (s, 0, 0)),
            scratch_shapes=[pltpu.VMEM((OG * SLOTS * HALF, TILES * HALF * OG), jnp.bfloat16)],
        ),
        out_shape=jax.ShapeDtypeStruct((orbitals, kept, width), jnp.bfloat16),
    )(code, tiled)


def gram_kernel(first_ref, x_ref, *refs):
    outs, acc = refs[:-1], refs[-1]
    step = pl.program_id(0)
    x = x_ref[...]
    part = lax.dot_general(x, x, (((0,), (0,)), ((), ())), preferred_element_type=jnp.float32)

    @pl.when(step == 0)
    def _():
        acc[...] = part

    @pl.when(step > 0)
    def _():
        acc[...] += part

    @pl.when(step == pl.num_programs(0) - 1)
    def _():
        share = acc.shape[0] // SHARES
        for j in range(SHARES):
            start = pl.multiple_of(((first_ref[0] + j) % SHARES) * share, share)
            outs[j][...] = acc[pl.ds(start, share), :]


def gram(first, columns, depth=1024):
    rows, width = columns.shape
    share = width // SHARES
    return pl.pallas_call(
        gram_kernel,
        grid_spec=pltpu.PrefetchScalarGridSpec(
            num_scalar_prefetch=1,
            grid=(rows // depth,),
            in_specs=[pl.BlockSpec((depth, width), lambda s, f: (s, 0))],
            out_specs=[pl.BlockSpec((share, width), lambda s, f: (0, 0))] * SHARES,
            scratch_shapes=[pltpu.VMEM((width, width), jnp.float32)],
        ),
        out_shape=[jax.ShapeDtypeStruct((share, width), jnp.float32)] * SHARES,
    )(first, columns)


def slot_codes(screen):
    seen = jnp.zeros_like(screen[0])
    codes = [jnp.full_like(screen[0], NONE) for _ in range(SLOTS)]
    inner = lax.iota(jnp.int32, screen.shape[1]) % OG
    for t in range(TILES):
        kept = screen[t] == 1
        for k in range(SLOTS):
            codes[k] = jnp.where(kept & (seen == k), t * HALF * OG + inner, codes[k])
        seen = seen + screen[t]
    return jnp.stack(codes)


def per_device(half_blocks, screen, domain_length, domain_index, orbital_coeff):
    dom_width = half_blocks.shape[2]
    packed = pack(slot_codes(screen), half_blocks)
    arrived = lax.all_to_all(packed, ("y", "x", "zl", "c"), split_axis=0, concat_axis=0, tiled=True)
    columns = arrived.reshape(-1, dom_width)
    shares = gram(lax.axis_index("zh").reshape(1), columns)
    total = None
    for j, share in enumerate(shares):
        route = [(g * 4 + x, x * 4 + (g + j) % 4) for g in range(4) for x in range(4)]
        got = lax.ppermute(share, ("zh", "x"), route)
        total = got if total is None else total + got
    row_share = dom_width // SHARES
    length = domain_length[0]
    row_place = lax.axis_index("x") * row_share + lax.iota(jnp.int32, row_share)
    col_place = lax.iota(jnp.int32, dom_width)
    inside = ((row_place < length)[:, None] & (col_place < length)[None, :]).astype(jnp.float32)
    exch_rows = total * inside
    local_coeff = jnp.take(orbital_coeff, domain_index[0], axis=0).astype(jnp.float32)
    occ_rows = jnp.einsum("ab,bj->ja", exch_rows, local_coeff, precision=lax.Precision.HIGHEST)
    return (exch_rows[None], occ_rows[None])


def solution(mesh):
    split = Mesh(mesh.devices.reshape(4, 4, 2, 2, 4), ("y", "zh", "zl", "c", "x"))
    aux = ("y", "zh", "zl", "c")
    every = aux + ("x",)
    return jax.shard_map(
        per_device,
        mesh=split,
        in_specs=(P(every, None, None), P(every, None), P(aux), P(aux, None), P()),
        out_specs=(P(aux, "x", None), P(aux, None, "x")),
        check_vma=False,
    )
```

time: 170 us -> 162 us (0.953)
  the two profiles are of different devices: /device:TPU:3 before, /device:TPU:37 now
where the time goes in v1:
time: 162 us; the launch traced here: 161 us
  waiting for transfers between devices  110 us (68%)
  starting transfers between devices  19.9 us (12%)
  Pallas kernels  15.8 us (10%)
  local copies, waits for them, and re-layouts  8.29 us (5%)
  other arithmetic  4.66 us (3%)
    ppermute x4, waiting for transfers between devices, per_device(): got = lax.ppermute(share, ('zh', 'x'), route)  57.2 us
    all_to_all x1, waiting for transfers between devices, per_device(): lax.all_to_all(packed, ('y', 'x', 'zl', 'c'), split_axis=0, concat_axis=0...  52.8 us
    ppermute x4, starting transfers between devices, per_device(): got = lax.ppermute(share, ('zh', 'x'), route)  10.4 us
    pallas_call x1, Pallas kernels, pack(): pl.pallas_call(pack_kernel, grid_spec=pltpu.PrefetchScalarGridSpec(num_sc...  9.7 us
    all_to_all x1, starting transfers between devices, per_device(): lax.all_to_all(packed, ('y', 'x', 'zl', 'c'), split_axis=0, concat_axis=0...  9.5 us
    pallas_call x1, Pallas kernels, gram(): pl.pallas_call(gram_kernel, grid_spec=pltpu.PrefetchScalarGridSpec(num_sc...  6.06 us
    gather x1, local copies, waits for them, and re-layouts, per_device(): jnp.take(orbital_coeff, domain_index[0], axis=0).astype(jnp.float32)  4.17 us
    unnamed x7, local copies, waits for them, and re-layouts  4.13 us
  transfers between devices with their start and end apart: 5, of which 3 were waited for; matrix products, arithmetic and copies ran while one was open for 5% of the time, Pallas kernels for 0%

profile of v1, /device:TPU:37, one launch (start us, length us, event | category | flops | bytes accessed | tf_op | source)
XLA Modules:
  0.0 161.1 jit_solution(6390349058628559733)
XLA Ops:
  0.6 1.0 and_select_fusion.28
  1.6 1.0 and_select_fusion.20
  2.6 1.0 and_select_fusion.6
  3.6 0.6 pad_add_fusion.code_ref
  4.2 9.7 %shard_map.68 = bf16[64,64,512]{2,1,0:T(8,128)(2,1)} custom-call(s32[4,64]{1,0:T(4,128)} %pad_add_fusion.code_ref, bf16[8,2,8,64,512]{4,3,2,1,0:T(8,128)(2,1)} %bitcast.14), custom_call_target="tpu_custom_call" | custom-call | tf_op jit(solution)/shard_map/pallas_call | solution.py:42
  13.9 9.5 %all-to-all-start = ((bf16[64,64,512]{2,1,0:T(8,128)(2,1)}), bf16[64,64,512]{2,1,0:T(8,128)(2,1)}, u32[]{:S(2)}, u32[]{:S(2)}) async-start(bf16[64,64,512]{2,1,0:T(8,128)(2,1)} %shard_map.68), calls=%async_computation | async-start | bytes 8388608 | tf_op jit(solution)/shard_map/all_to_all | solution.py:108
  24.1 0.0 copy-done.2
  24.1 52.8 %all-to-all-done = bf16[64,64,512]{2,1,0:T(8,128)(2,1)} async-done(((bf16[64,64,512]{2,1,0:T(8,128)(2,1)}), bf16[64,64,512]{2,1,0:T(8,128)(2,1)}, u32[]{:S(2)}, u32[]{:S(2)}) %all-to-all-start) | async-done | bytes 4194336 | tf_op jit(solution)/shard_map/all_to_all | solution.py:108
  77.0 6.1 %shard_map.69 = (f32[128,512]{1,0:T(8,128)}, f32[128,512]{1,0:T(8,128)}, f32[128,512]{1,0:T(8,128)}, f32[128,512]{1,0:T(8,128)}) custom-call(s32[1]{0:T(128)} %bitcast.1.first_ref, bf16[4096,512]{1,0:T(8,128)(2,1)} %bitcast.3.x_ref), custom_call_target="tpu_custom_call" | custom-call | tf_op jit(solution)/shard_map/pallas_call | solution.py:80
  83.0 8.5 %collective-permute-start = (f32[128,512]{1,0:T(8,128)}, f32[128,512]{1,0:T(8,128)S(1)}, u32[]{:S(2)}, u32[]{:S(2)}) collective-permute-start(f32[128,512]{1,0:T(8,128)} %get-tuple-element.6), channel_id=1, source_target_pairs={{0,0},{1,16},{2,32},{3,48},{16,1},{17,17},{18,33},{19,49},{32,2},{... | collective-permute-start | bytes 786440 | tf_op jit(solution)/shard_map/ppermute | solution.py:114
  91.5 0.7 collective-permute-start.1
  92.2 1.2 collective-permute-start.2
  93.4 0.1 collective-permute-start.3
  93.5 0.0 copy-done
  93.5 4.1 %copy.8 = bf16[20000,64]{1,0:T(8,128)(2,1)} copy(bf16[20000,64]{0,1:T(8,128)(2,1)S(1)} %copy-done) | data formatting | bytes 5120000 | tf_op args[4]
  97.6 4.2 %gather_fusion = bf16[512,64]{1,0:T(8,128)(2,1)S(1)} fusion(bf16[20000,64]{1,0:T(8,128)(2,1)} %copy.8, s32[1024]{0:T(1024)S(1)} %pad_clamp_fusion), kind=kCustom, calls=%fused_computation | custom fusion | bytes 133120 | tf_op jit(solution)/shard_map/jit(_take)/gather | solution.py:122
  101.8 0.0 collective-permute-done
  101.8 20.6 %collective-permute-done.1 = f32[128,512]{1,0:T(8,128)S(1)} collective-permute-done((f32[128,512]{1,0:T(8,128)}, f32[128,512]{1,0:T(8,128)S(1)}, u32[]{:S(2)}, u32[]{:S(2)}) %collective-permute-start.1) | collective-permute-done | bytes 262176 | tf_op jit(solution)/shard_map/ppermute | solution.py:114
  122.4 0.0 collective-permute-done.2
  122.4 36.6 %collective-permute-done.3 = f32[128,512]{1,0:T(8,128)} collective-permute-done((f32[128,512]{1,0:T(8,128)}, f32[128,512]{1,0:T(8,128)}, u32[]{:S(2)}, u32[]{:S(2)}) %collective-permute-start.3) | collective-permute-done | bytes 262176 | tf_op jit(solution)/shard_map/ppermute | solution.py:114
  159.0 1.1 add_select_fusion
  160.0 0.0 copy-start.1
  160.1 1.0 convolution_bitcast_fusion
  161.1 0.0 copy-done.1
  (7 shorter events, 0.0 us)
Async XLA Ops:
  13.9 10.2 %copy-start.2 = (s32[1,512]{1,0:T(1,128)S(1)}, s32[1,512]{1,0:T(1,128)}, u32[]{:S(2)}) copy-start(s32[1,512]{1,0:T(1,128)} %param.8) | copy-start | bytes 6148
  13.9 79.6 %copy-start = (bf16[20000,64]{0,1:T(8,128)(2,1)S(1)}, bf16[20000,64]{0,1:T(8,128)(2,1)}, u32[]{:S(2)}) copy-start(bf16[20000,64]{0,1:T(8,128)(2,1)} %param.9) | copy-start | bytes 7680004
  13.9 63.1 %all-to-all-start = ((bf16[64,64,512]{2,1,0:T(8,128)(2,1)}), bf16[64,64,512]{2,1,0:T(8,128)(2,1)}, u32[]{:S(2)}, u32[]{:S(2)}) async-start(bf16[64,64,512]{2,1,0:T(8,128)(2,1)} %shard_map.68), calls=%async_computation | async-start | bytes 8388608 | tf_op jit(solution)/shard_map/all_to_all | solution.py:108
  83.0 18.8 %collective-permute-start = (f32[128,512]{1,0:T(8,128)}, f32[128,512]{1,0:T(8,128)S(1)}, u32[]{:S(2)}, u32[]{:S(2)}) collective-permute-start(f32[128,512]{1,0:T(8,128)} %get-tuple-element.6), channel_id=1, source_target_pairs={{0,0},{1,16},{2,32},{3,48},{16,1},{17,17},{18,33},{19,49},{32,2},{... | collective-permute-start | bytes 786440 | tf_op jit(solution)/shard_map/ppermute | solution.py:114
  91.5 30.9 %collective-permute-start.1 = (f32[128,512]{1,0:T(8,128)}, f32[128,512]{1,0:T(8,128)S(1)}, u32[]{:S(2)}, u32[]{:S(2)}) collective-permute-start(f32[128,512]{1,0:T(8,128)} %get-tuple-element.7), channel_id=1, source_target_pairs={{0,1},{1,17},{2,33},{3,49},{16,2},{17,18},{18,34},{19,50},{32,3},{... | collective-permute-start | bytes 786440 | tf_op jit(solution)/shard_map/ppermute | solution.py:114
  92.2 30.2 %collective-permute-start.2 = (f32[128,512]{1,0:T(8,128)}, f32[128,512]{1,0:T(8,128)S(1)}, u32[]{:S(2)}, u32[]{:S(2)}) collective-permute-start(f32[128,512]{1,0:T(8,128)} %get-tuple-element.8), channel_id=1, source_target_pairs={{0,2},{1,18},{2,34},{3,50},{16,3},{17,19},{18,35},{19,51},{32,0},{... | collective-permute-start | bytes 786440 | tf_op jit(solution)/shard_map/ppermute | solution.py:114
  93.4 65.6 %collective-permute-start.3 = (f32[128,512]{1,0:T(8,128)}, f32[128,512]{1,0:T(8,128)}, u32[]{:S(2)}, u32[]{:S(2)}) collective-permute-start(f32[128,512]{1,0:T(8,128)} %get-tuple-element.9), channel_id=1, source_target_pairs={{0,3},{1,19},{2,35},{3,51},{16,0},{17,16},{18,32},{19,48},{32,1},{... | collective-permute-start | bytes 786440 | tf_op jit(solution)/shard_map/ppermute | solution.py:114
  160.0 1.0 copy-start.1

commit v2 on v1

--- a/solution.py
+++ b/solution.py
@@ -8,48 +8,72 @@
 
 TILES = 8
 SLOTS = 4
-TROWS = 16
-HALF = 8
-OG = 8
+PART = 4
+PARTS = 4
+OG = 16
 SHARES = 4
 NONE = -1000
 
 
-def pack_kernel(code_ref, x_ref, o_ref, pick_ref):
-    step = pl.program_id(0)
-    width = TILES * HALF * OG
-    place = lax.broadcasted_iota(jnp.int32, (HALF, width), 1) - OG * lax.broadcasted_iota(
-        jnp.int32, (HALF, width), 0
-    )
-    for i in range(OG):
-        for k in range(0, SLOTS, 2):
-            pair = [
-                jnp.where(place == code_ref[k + d, step * OG + i], 1.0, 0.0) for d in range(2)
-            ]
-            row = (i * SLOTS + k) * HALF
-            pick_ref[row : row + 2 * HALF, :] = jnp.concatenate(pair, axis=0).astype(jnp.bfloat16)
-    for h in range(2):
-        rows = x_ref[:, h].astype(jnp.float32).reshape(width, x_ref.shape[-1]).astype(jnp.bfloat16)
-        got = jnp.dot(pick_ref[...], rows, preferred_element_type=jnp.float32)
-        got = got.astype(jnp.bfloat16).reshape(OG, SLOTS * HALF, x_ref.shape[-1])
-        o_ref[:, h * SLOTS * HALF : (h + 1) * SLOTS * HALF, :] = got
+def code_kernel(screen_ref, o_ref):
+    seen = jnp.zeros_like(screen_ref[0:1, :])
+    inner = lax.broadcasted_iota(jnp.int32, seen.shape, 1) % OG
+    codes = [jnp.full_like(seen, NONE) for _ in range(SLOTS)]
+    for t in range(TILES):
+        kept = screen_ref[t : t + 1, :]
+        for k in range(SLOTS):
+            here = (kept == 1) & (seen == k)
+            codes[k] = jnp.where(here, t * PART * OG + inner, codes[k])
+        seen = seen + kept
+    for k in range(SLOTS):
+        o_ref[k : k + 1, :] = codes[k]
 
 
-def pack(code, half_blocks):
+def slot_codes(screen):
+    return pl.pallas_call(
+        code_kernel, out_shape=jax.ShapeDtypeStruct((SLOTS, screen.shape[1]), jnp.int32)
+    )(screen)
+
+
+def pack_kernel(code_ref, group_ref, x_ref, o_ref, pick_ref):
+    step = pl.program_id(0)
+    width = TILES * PART * OG
+    row = lax.broadcasted_iota(jnp.int32, (2 * PART, width), 0)
+    place = lax.broadcasted_iota(jnp.int32, (2 * PART, width), 1) - OG * (row % PART)
+    for i in range(OG):
+        both = []
+        for k in range(0, SLOTS, 2):
+            first, second = (code_ref[k + d, step * OG + i] for d in range(2))
+            both.append(jnp.where(place == jnp.where(row < PART, first, second), 1.0, 0.0))
+        at = i * SLOTS * PART
+        pick_ref[at : at + SLOTS * PART, :] = jnp.concatenate(both, axis=0).astype(jnp.bfloat16)
+    for h in range(PARTS):
+        rows = x_ref[:, h].reshape(width, x_ref.shape[-1])
+        got = jnp.dot(pick_ref[...], rows, preferred_element_type=jnp.float32).astype(jnp.bfloat16)
+        for i in range(OG):
+            low = i % 4
+            slot = ((i // 4 - low - group_ref[0] + 8) % 4) * 4 + low
+            at = i * SLOTS * PART
+            o_ref[slot, h * SLOTS * PART : (h + 1) * SLOTS * PART, :] = got[at : at + SLOTS * PART]
+
+
+def pack(code, group, half_blocks):
     rows, orbitals, width = half_blocks.shape
-    tiled = half_blocks.reshape(TILES, 2, HALF, orbitals, width)
+    tiled = half_blocks.reshape(TILES, PARTS, PART, orbitals, width)
     kept = rows // TILES * SLOTS
     return pl.pallas_call(
         pack_kernel,
         grid_spec=pltpu.PrefetchScalarGridSpec(
-            num_scalar_prefetch=1,
+            num_scalar_prefetch=2,
             grid=(orbitals // OG,),
-            in_specs=[pl.BlockSpec((TILES, 2, HALF, OG, width), lambda s, c: (0, 0, 0, s, 0))],
-            out_specs=pl.BlockSpec((OG, kept, width), lambda s, c: (s, 0, 0)),
-            scratch_shapes=[pltpu.VMEM((OG * SLOTS * HALF, TILES * HALF * OG), jnp.bfloat16)],
+            in_specs=[
+                pl.BlockSpec((TILES, PARTS, PART, OG, width), lambda s, c, g: (0, 0, 0, s, 0))
+            ],
+            out_specs=pl.BlockSpec((OG, kept, width), lambda s, c, g: (s, 0, 0)),
+            scratch_shapes=[pltpu.VMEM((OG * SLOTS * PART, TILES * PART * OG), jnp.bfloat16)],
         ),
         out_shape=jax.ShapeDtypeStruct((orbitals, kept, width), jnp.bfloat16),
-    )(code, tiled)
+    )(code, group, tiled)
 
 
 def gram_kernel(first_ref, x_ref, *refs):
@@ -90,28 +114,26 @@
     )(first, columns)
 
 
-def slot_codes(screen):
-    seen = jnp.zeros_like(screen[0])
-    codes = [jnp.full_like(screen[0], NONE) for _ in range(SLOTS)]
-    inner = lax.iota(jnp.int32, screen.shape[1]) % OG
-    for t in range(TILES):
-        kept = screen[t] == 1
-        for k in range(SLOTS):
-            codes[k] = jnp.where(kept & (seen == k), t * HALF * OG + inner, codes[k])
-        seen = seen + screen[t]
-    return jnp.stack(codes)
+def routes(j):
+    pairs = []
+    for g in range(4):
+        for low in range(4):
+            for x in range(4):
+                owner = (x + g + low) % 4
+                pairs.append(((g * 4 + low) * 4 + x, (owner * 4 + low) * 4 + (x + j) % 4))
+    return pairs
 
 
 def per_device(half_blocks, screen, domain_length, domain_index, orbital_coeff):
     dom_width = half_blocks.shape[2]
-    packed = pack(slot_codes(screen), half_blocks)
+    group = lax.axis_index("zh").reshape(1)
+    packed = pack(slot_codes(screen), group, half_blocks)
     arrived = lax.all_to_all(packed, ("y", "x", "zl", "c"), split_axis=0, concat_axis=0, tiled=True)
     columns = arrived.reshape(-1, dom_width)
-    shares = gram(lax.axis_index("zh").reshape(1), columns)
+    shares = gram(lax.axis_index("x").reshape(1), columns)
     total = None
     for j, share in enumerate(shares):
-        route = [(g * 4 + x, x * 4 + (g + j) % 4) for g in range(4) for x in range(4)]
-        got = lax.ppermute(share, ("zh", "x"), route)
+        got = lax.ppermute(share, ("zh", "zl", "c", "x"), routes(j))
         total = got if total is None else total + got
     row_share = dom_width // SHARES
     length = domain_length[0]

time: 162 us -> 125 us (0.77)
  the two profiles are of different devices: /device:TPU:37 before, /device:TPU:54 now
where the time goes in v2:
time: 125 us
  waiting for transfers between devices  71.8 us (57%)
  starting transfers between devices  26 us (21%)
  Pallas kernels  15.2 us (12%)
  local copies, waits for them, and re-layouts  8.26 us (7%)
  between operations  1.38 us (1%)
    all_to_all x1, waiting for transfers between devices, per_device(): lax.all_to_all(packed, ('y', 'x', 'zl', 'c'), split_axis=0, concat_axis=0...  47.9 us
    ppermute x4, waiting for transfers between devices, per_device(): got = lax.ppermute(share, ('zh', 'zl', 'c', 'x'), routes(j))  23.9 us
    ppermute x4, starting transfers between devices, per_device(): got = lax.ppermute(share, ('zh', 'zl', 'c', 'x'), routes(j))  16.8 us
    all_to_all x1, starting transfers between devices, per_device(): lax.all_to_all(packed, ('y', 'x', 'zl', 'c'), split_axis=0, concat_axis=0...  9.15 us
    pallas_call x1, Pallas kernels, pack(): pl.pallas_call(pack_kernel, grid_spec=pltpu.PrefetchScalarGridSpec(num_sc...  7.87 us
    pallas_call x1, Pallas kernels, gram(): pl.pallas_call(gram_kernel, grid_spec=pltpu.PrefetchScalarGridSpec(num_sc...  6.06 us
    gather x1, local copies, waits for them, and re-layouts, per_device(): jnp.take(orbital_coeff, domain_index[0], axis=0).astype(jnp.float32)  4.16 us
    unnamed x7, local copies, waits for them, and re-layouts  4.1 us
  transfers between devices with their start and end apart: 5, of which 3 were waited for; matrix products, arithmetic and copies ran while one was open for 7% of the time, Pallas kernels for 0%

profile of v2, /device:TPU:54, one launch (start us, length us, event | category | flops | bytes accessed | tf_op | source)
XLA Modules:
  0.0 124.8 jit_solution(6712440481662595003)
XLA Ops:
  0.6 1.3 %shard_map.68.code_ref = s32[4,64]{1,0:T(4,128)} custom-call(s32[8,64]{1,0:T(8,128)} %screen_ref.1), custom_call_target="tpu_custom_call" | custom-call | tf_op jit(solution)/shard_map/pallas_call | solution.py:33
  1.9 7.9 %shard_map.69 = bf16[64,64,512]{2,1,0:T(8,128)(2,1)} custom-call(s32[4,64]{1,0:T(4,128)} %shard_map.68.code_ref, s32[1]{0:T(128)} %bitcast.2.group_ref, bf16[8,4,4,64,512]{4,3,2,1,0:T(8,128)(2,1)} %bitcast.15), custom_call_target="tpu_custom_call" | custom-call | tf_op jit(solution)/shard_map/pallas_call | solution.py:64
  9.8 0.0 copy-start.2
  9.8 0.0 copy-start
  9.8 9.2 %all-to-all-start = ((bf16[64,64,512]{2,1,0:T(8,128)(2,1)}), bf16[64,64,512]{2,1,0:T(8,128)(2,1)}, u32[]{:S(2)}, u32[]{:S(2)}) async-start(bf16[64,64,512]{2,1,0:T(8,128)(2,1)} %shard_map.69), calls=%async_computation | async-start | bytes 8388608 | tf_op jit(solution)/shard_map/all_to_all | solution.py:131
  19.6 0.0 copy-done.2
  19.7 47.9 %all-to-all-done = bf16[64,64,512]{2,1,0:T(8,128)(2,1)} async-done(((bf16[64,64,512]{2,1,0:T(8,128)(2,1)}), bf16[64,64,512]{2,1,0:T(8,128)(2,1)}, u32[]{:S(2)}, u32[]{:S(2)}) %all-to-all-start) | async-done | bytes 4194336 | tf_op jit(solution)/shard_map/all_to_all | solution.py:131
  67.6 6.1 %shard_map.70 = (f32[128,512]{1,0:T(8,128)}, f32[128,512]{1,0:T(8,128)}, f32[128,512]{1,0:T(8,128)}, f32[128,512]{1,0:T(8,128)}) custom-call(s32[1]{0:T(128)} %bitcast.1.first_ref, bf16[4096,512]{1,0:T(8,128)(2,1)} %bitcast.4.x_ref), custom_call_target="tpu_custom_call" | custom-call | tf_op jit(solution)/shard_map/pallas_call | solution.py:104
  73.7 5.2 %collective-permute-start = (f32[128,512]{1,0:T(8,128)}, f32[128,512]{1,0:T(8,128)S(1)}, u32[]{:S(2)}, u32[]{:S(2)}) collective-permute-start(f32[128,512]{1,0:T(8,128)} %get-tuple-element.6), channel_id=1, source_target_pairs={{0,0},{1,17},{2,34},{3,51},{4,20},{5,37},{6,54},{7,7},{8,40},{9,57... | collective-permute-start | bytes 786440 | tf_op jit(solution)/shard_map/ppermute | solution.py:136
  78.8 10.7 %collective-permute-start.1 = (f32[128,512]{1,0:T(8,128)}, f32[128,512]{1,0:T(8,128)S(1)}, u32[]{:S(2)}, u32[]{:S(2)}) collective-permute-start(f32[128,512]{1,0:T(8,128)} %get-tuple-element.7), channel_id=1, source_target_pairs={{0,1},{1,18},{2,35},{3,48},{4,21},{5,38},{6,55},{7,4},{8,41},{9,58... | collective-permute-start | bytes 786440 | tf_op jit(solution)/shard_map/ppermute | solution.py:136
  89.6 0.0 collective-permute-start.2
  89.6 0.9 collective-permute-start.3
  90.5 0.0 copy-done
  90.5 4.1 %copy.8 = bf16[20000,64]{1,0:T(8,128)(2,1)} copy(bf16[20000,64]{0,1:T(8,128)(2,1)S(1)} %copy-done) | data formatting | bytes 5120000 | tf_op args[4]
  94.6 4.2 %gather_fusion = bf16[512,64]{1,0:T(8,128)(2,1)S(1)} fusion(bf16[20000,64]{1,0:T(8,128)(2,1)} %copy.8, s32[1024]{0:T(1024)S(1)} %pad_clamp_fusion), kind=kCustom, calls=%fused_computation | custom fusion | bytes 133120 | tf_op jit(solution)/shard_map/jit(_take)/gather | solution.py:144
  98.8 0.0 collective-permute-done
  98.8 0.0 collective-permute-done.1
  98.8 0.7 collective-permute-done.2
  99.6 23.1 %collective-permute-done.3 = f32[128,512]{1,0:T(8,128)} collective-permute-done((f32[128,512]{1,0:T(8,128)}, f32[128,512]{1,0:T(8,128)}, u32[]{:S(2)}, u32[]{:S(2)}) %collective-permute-start.3) | collective-permute-done | bytes 262176 | tf_op jit(solution)/shard_map/ppermute | solution.py:136
  122.7 1.1 add_select_fusion
  123.8 0.0 copy-start.1
  123.8 1.0 convolution_bitcast_fusion
  124.8 0.0 copy-done.1
  (5 shorter events, 0.0 us)
Async XLA Ops:
  9.8 9.8 %copy-start.2 = (s32[1,512]{1,0:T(1,128)S(1)}, s32[1,512]{1,0:T(1,128)}, u32[]{:S(2)}) copy-start(s32[1,512]{1,0:T(1,128)} %param.8) | copy-start | bytes 6148
  9.8 80.7 %copy-start = (bf16[20000,64]{0,1:T(8,128)(2,1)S(1)}, bf16[20000,64]{0,1:T(8,128)(2,1)}, u32[]{:S(2)}) copy-start(bf16[20000,64]{0,1:T(8,128)(2,1)} %param.9) | copy-start | bytes 7680004
  9.8 57.8 %all-to-all-start = ((bf16[64,64,512]{2,1,0:T(8,128)(2,1)}), bf16[64,64,512]{2,1,0:T(8,128)(2,1)}, u32[]{:S(2)}, u32[]{:S(2)}) async-start(bf16[64,64,512]{2,1,0:T(8,128)(2,1)} %shard_map.69), calls=%async_computation | async-start | bytes 8388608 | tf_op jit(solution)/shard_map/all_to_all | solution.py:131
  73.7 25.1 %collective-permute-start = (f32[128,512]{1,0:T(8,128)}, f32[128,512]{1,0:T(8,128)S(1)}, u32[]{:S(2)}, u32[]{:S(2)}) collective-permute-start(f32[128,512]{1,0:T(8,128)} %get-tuple-element.6), channel_id=1, source_target_pairs={{0,0},{1,17},{2,34},{3,51},{4,20},{5,37},{6,54},{7,7},{8,40},{9,57... | collective-permute-start | bytes 786440 | tf_op jit(solution)/shard_map/ppermute | solution.py:136
  78.8 20.0 %collective-permute-start.1 = (f32[128,512]{1,0:T(8,128)}, f32[128,512]{1,0:T(8,128)S(1)}, u32[]{:S(2)}, u32[]{:S(2)}) collective-permute-start(f32[128,512]{1,0:T(8,128)} %get-tuple-element.7), channel_id=1, source_target_pairs={{0,1},{1,18},{2,35},{3,48},{4,21},{5,38},{6,55},{7,4},{8,41},{9,58... | collective-permute-start | bytes 786440 | tf_op jit(solution)/shard_map/ppermute | solution.py:136
  89.6 10.0 %collective-permute-start.2 = (f32[128,512]{1,0:T(8,128)}, f32[128,512]{1,0:T(8,128)S(1)}, u32[]{:S(2)}, u32[]{:S(2)}) collective-permute-start(f32[128,512]{1,0:T(8,128)} %get-tuple-element.8), channel_id=1, source_target_pairs={{0,2},{1,19},{2,32},{3,49},{4,22},{5,39},{6,52},{7,5},{8,42},{9,59... | collective-permute-start | bytes 786440 | tf_op jit(solution)/shard_map/ppermute | solution.py:136
  89.6 33.1 %collective-permute-start.3 = (f32[128,512]{1,0:T(8,128)}, f32[128,512]{1,0:T(8,128)}, u32[]{:S(2)}, u32[]{:S(2)}) collective-permute-start(f32[128,512]{1,0:T(8,128)} %get-tuple-element.9), channel_id=1, source_target_pairs={{0,3},{1,16},{2,33},{3,50},{4,23},{5,36},{6,53},{7,6},{8,43},{9,56... | collective-permute-start | bytes 786440 | tf_op jit(solution)/shard_map/ppermute | solution.py:136
  123.8 1.0 copy-start.1

commit v3 on v2

v3 whole, which is shorter than its diff:
```python
import jax
import jax.numpy as jnp
from jax import lax
from jax.experimental import pallas as pl
from jax.experimental.pallas import tpu as pltpu
from jax.sharding import Mesh
from jax.sharding import PartitionSpec as P

TILES = 8
SLOTS = 4
PART = 4
PARTS = 4
OG = 16
SHARES = 4
NONE = -1000


def code_kernel(screen_ref, o_ref):
    seen = jnp.zeros_like(screen_ref[0:1, :])
    inner = lax.broadcasted_iota(jnp.int32, seen.shape, 1) % OG
    codes = [jnp.full_like(seen, NONE) for _ in range(SLOTS)]
    for t in range(TILES):
        kept = screen_ref[t : t + 1, :]
        for k in range(SLOTS):
            here = (kept == 1) & (seen == k)
            codes[k] = jnp.where(here, t * PART * OG + inner, codes[k])
        seen = seen + kept
    for k in range(SLOTS):
        o_ref[k : k + 1, :] = codes[k]


def slot_codes(screen):
    return pl.pallas_call(
        code_kernel, out_shape=jax.ShapeDtypeStruct((SLOTS, screen.shape[1]), jnp.int32)
    )(screen)


def holder(zh, low, g):
    away = (zh - g) & 3
    return (away + 2 * (g & 1) * (1 - (away & 1)) - low) & 3


def pack_kernel(code_ref, group_ref, x_hbm, o_hbm, x_ref, o_ref, pick_ref, in_sems, out_sems):
    steps = x_hbm.shape[3] // OG
    arrivals = [
        pltpu.make_async_copy(
            x_hbm.at[:, :, :, s * OG : (s + 1) * OG, :], x_ref.at[s], in_sems.at[s]
        )
        for s in range(steps)
    ]
    leaving = [
        pltpu.make_async_copy(
            o_ref.at[s * OG : (s + 1) * OG], o_hbm.at[s * OG : (s + 1) * OG], out_sems.at[s]
        )
        for s in range(steps)
    ]
    for copy in arrivals:
        copy.start()
    slots = [holder(i // 4, i % 4, group_ref[0]) * 4 + i % 4 for i in range(OG)]
    width = TILES * PART * OG
    row = lax.broadcasted_iota(jnp.int32, (2 * PART, width), 0)
    place = lax.broadcasted_iota(jnp.int32, (2 * PART, width), 1) - OG * (row % PART)
    for s in range(steps):
        for i in range(OG):
            both = []
            for k in range(0, SLOTS, 2):
                first, second = (code_ref[k + d, s * OG + i] for d in range(2))
                both.append(jnp.where(place == jnp.where(row < PART, first, second), 1.0, 0.0))
            at = i * SLOTS * PART
            pick_ref[at : at + SLOTS * PART, :] = jnp.concatenate(both, axis=0).astype(jnp.bfloat16)
        arrivals[s].wait()
        for h in range(PARTS):
            rows = x_ref[s, :, h].reshape(width, x_ref.shape[-1])
            got = jnp.dot(pick_ref[...], rows, preferred_element_type=jnp.float32)
            got = got.astype(jnp.bfloat16)
            for i in range(OG):
                at = i * SLOTS * PART
                to = h * SLOTS * PART
                o_ref[s * OG + slots[i], to : to + SLOTS * PART, :] = got[at : at + SLOTS * PART]
        leaving[s].start()
    for copy in leaving:
        copy.wait()


def pack(code, group, half_blocks):
    rows, orbitals, width = half_blocks.shape
    tiled = half_blocks.reshape(TILES, PARTS, PART, orbitals, width)
    kept = rows // TILES * SLOTS
    steps = orbitals // OG
    return pl.pallas_call(
        pack_kernel,
        in_specs=[
            pl.BlockSpec(memory_space=pltpu.SMEM),
            pl.BlockSpec(memory_space=pltpu.SMEM),
            pl.BlockSpec(memory_space=pl.ANY),
        ],
        out_specs=pl.BlockSpec(memory_space=pl.ANY),
        out_shape=jax.ShapeDtypeStruct((orbitals, kept, width), jnp.bfloat16),
        scratch_shapes=[
            pltpu.VMEM((steps, TILES, PARTS, PART, OG, width), jnp.bfloat16),
            pltpu.VMEM((orbitals, kept, width), jnp.bfloat16),
            pltpu.VMEM((OG * SLOTS * PART, TILES * PART * OG), jnp.bfloat16),
            pltpu.SemaphoreType.DMA((steps,)),
            pltpu.SemaphoreType.DMA((steps,)),
        ],
    )(code, group, tiled)


def gram_kernel(first_ref, x_hbm, *refs):
    outs, x_ref, acc, sems = refs[:SHARES], refs[-3], refs[-2], refs[-1]
    parts = sems.shape[0]
    depth = x_hbm.shape[0] // parts
    arrivals = [
        pltpu.make_async_copy(
            x_hbm.at[p * depth : (p + 1) * depth], x_ref.at[p * depth : (p + 1) * depth], sems.at[p]
        )
        for p in range(parts)
    ]
    for copy in arrivals:
        copy.start()
    for p in range(parts):
        arrivals[p].wait()
        x = x_ref[p * depth : (p + 1) * depth, :]
        part = lax.dot_general(x, x, (((0,), (0,)), ((), ())), preferred_element_type=jnp.float32)
        if p == 0:
            acc[...] = part
        else:
            acc[...] += part
    share = acc.shape[0] // SHARES
    for j in range(SHARES):
        start = pl.multiple_of(((first_ref[0] + j) % SHARES) * share, share)
        outs[j][...] = acc[pl.ds(start, share), :]


def gram(first, columns, parts=4):
    rows, width = columns.shape
    share = width // SHARES
    return pl.pallas_call(
        gram_kernel,
        in_specs=[pl.BlockSpec(memory_space=pltpu.SMEM), pl.BlockSpec(memory_space=pl.ANY)],
        out_specs=[pl.BlockSpec(memory_space=pltpu.VMEM)] * SHARES,
        out_shape=[jax.ShapeDtypeStruct((share, width), jnp.float32)] * SHARES,
        scratch_shapes=[
            pltpu.VMEM((rows, width), jnp.bfloat16),
            pltpu.VMEM((width, width), jnp.float32),
            pltpu.SemaphoreType.DMA((parts,)),
        ],
    )(first, columns)


def routes(j):
    pairs = []
    for g in range(4):
        for low in range(4):
            for owner in range(4):
                x = holder(owner, low, g)
                pairs.append(((g * 4 + low) * 4 + x, (owner * 4 + low) * 4 + (x + j) % 4))
    return pairs


def per_device(half_blocks, screen, domain_length, domain_index, orbital_coeff):
    dom_width = half_blocks.shape[2]
    group = lax.axis_index("zh").reshape(1)
    packed = pack(slot_codes(screen), group, half_blocks)
    arrived = lax.all_to_all(packed, ("y", "x", "zl", "c"), split_axis=0, concat_axis=0, tiled=True)
    columns = arrived.reshape(-1, dom_width)
    shares = gram(lax.axis_index("x").reshape(1), columns)
    total = None
    for j, share in enumerate(shares):
        got = lax.ppermute(share, ("zh", "zl", "c", "x"), routes(j))
        total = got if total is None else total + got
    row_share = dom_width // SHARES
    length = domain_length[0]
    row_place = lax.axis_index("x") * row_share + lax.iota(jnp.int32, row_share)
    col_place = lax.iota(jnp.int32, dom_width)
    inside = ((row_place < length)[:, None] & (col_place < length)[None, :]).astype(jnp.float32)
    exch_rows = total * inside
    local_coeff = jnp.take(orbital_coeff, domain_index[0], axis=0).astype(jnp.float32)
    occ_rows = jnp.einsum("ab,bj->ja", exch_rows, local_coeff, precision=lax.Precision.HIGHEST)
    return (exch_rows[None], occ_rows[None])


def solution(mesh):
    split = Mesh(mesh.devices.reshape(4, 4, 2, 2, 4), ("y", "zh", "zl", "c", "x"))
    aux = ("y", "zh", "zl", "c")
    every = aux + ("x",)
    return jax.shard_map(
        per_device,
        mesh=split,
        in_specs=(P(every, None, None), P(every, None), P(aux), P(aux, None), P()),
        out_specs=(P(aux, "x", None), P(aux, None, "x")),
        check_vma=False,
    )
```

time: 125 us -> 117 us (0.936)
  the two profiles are of different devices: /device:TPU:54 before, /device:TPU:52 now
where the time goes in v3:
time: 117 us
  waiting for transfers between devices  67.6 us (58%)
  starting transfers between devices  25.3 us (22%)
  Pallas kernels  12.5 us (11%)
  local copies, waits for them, and re-layouts  8.27 us (7%)
  between operations  1.41 us (1%)
    all_to_all x1, waiting for transfers between devices, per_device(): lax.all_to_all(packed, ('y', 'x', 'zl', 'c'), split_axis=0, concat_axis=0...  52.5 us
    ppermute x4, starting transfers between devices, per_device(): got = lax.ppermute(share, ('zh', 'zl', 'c', 'x'), routes(j))  16.1 us
    ppermute x4, waiting for transfers between devices, per_device(): got = lax.ppermute(share, ('zh', 'zl', 'c', 'x'), routes(j))  15.1 us
    all_to_all x1, starting transfers between devices, per_device(): lax.all_to_all(packed, ('y', 'x', 'zl', 'c'), split_axis=0, concat_axis=0...  9.16 us
    pallas_call x1, Pallas kernels, pack(): pl.pallas_call(pack_kernel, in_specs=[pl.BlockSpec(memory_space=pltpu.SME...  6.35 us
    pallas_call x1, Pallas kernels, gram(): pl.pallas_call(gram_kernel, in_specs=[pl.BlockSpec(memory_space=pltpu.SME...  4.84 us
    gather x1, local copies, waits for them, and re-layouts, per_device(): jnp.take(orbital_coeff, domain_index[0], axis=0).astype(jnp.float32)  4.16 us
    unnamed x7, local copies, waits for them, and re-layouts  4.11 us
  transfers between devices with their start and end apart: 5, of which 3 were waited for; matrix products, arithmetic and copies ran while one was open for 7% of the time, Pallas kernels for 0%

profile of v3, /device:TPU:52, one launch (start us, length us, event | category | flops | bytes accessed | tf_op | source)
XLA Modules:
  0.0 117.1 jit_solution(435842406094825418)
XLA Ops:
  0.6 1.3 %shard_map.68.code_ref = s32[4,64]{1,0:T(4,128)} custom-call(s32[8,64]{1,0:T(8,128)} %screen_ref.1), custom_call_target="tpu_custom_call" | custom-call | tf_op jit(solution)/shard_map/pallas_call | solution.py:33
  1.9 6.4 %shard_map.69 = bf16[64,64,512]{2,1,0:T(8,128)(2,1)} custom-call(s32[4,64]{1,0:T(4,128)} %shard_map.68.code_ref, s32[1]{0:T(128)} %bitcast.2.group_ref, bf16[8,4,4,64,512]{4,3,2,1,0:T(8,128)(2,1)} %bitcast.15), custom_call_target="tpu_custom_call" | custom-call | tf_op jit(solution)/shard_map/pallas_call | solution.py:90
  8.3 0.0 copy-start.2
  8.3 0.0 copy-start
  8.3 9.2 %all-to-all-start = ((bf16[64,64,512]{2,1,0:T(8,128)(2,1)}), bf16[64,64,512]{2,1,0:T(8,128)(2,1)}, u32[]{:S(2)}, u32[]{:S(2)}) async-start(bf16[64,64,512]{2,1,0:T(8,128)(2,1)} %shard_map.69), calls=%async_computation | async-start | bytes 8388608 | tf_op jit(solution)/shard_map/all_to_all | solution.py:165
  18.1 0.0 copy-done.2
  18.2 52.5 %all-to-all-done = bf16[64,64,512]{2,1,0:T(8,128)(2,1)} async-done(((bf16[64,64,512]{2,1,0:T(8,128)(2,1)}), bf16[64,64,512]{2,1,0:T(8,128)(2,1)}, u32[]{:S(2)}, u32[]{:S(2)}) %all-to-all-start) | async-done | bytes 4194336 | tf_op jit(solution)/shard_map/all_to_all | solution.py:165
  70.7 4.8 %shard_map.70 = (f32[128,512]{1,0:T(8,128)}, f32[128,512]{1,0:T(8,128)}, f32[128,512]{1,0:T(8,128)}, f32[128,512]{1,0:T(8,128)}) custom-call(s32[1]{0:T(128)} %bitcast.1.first_ref, bf16[4096,512]{1,0:T(8,128)(2,1)} %bitcast.4.x_hbm), custom_call_target="tpu_custom_call" | custom-call | tf_op jit(solution)/shard_map/pallas_call | solution.py:138
  75.6 1.6 %collective-permute-start = (f32[128,512]{1,0:T(8,128)}, f32[128,512]{1,0:T(8,128)S(1)}, u32[]{:S(2)}, u32[]{:S(2)}) collective-permute-start(f32[128,512]{1,0:T(8,128)} %get-tuple-element.6), channel_id=1, source_target_pairs={{0,0},{1,17},{2,34},{3,51},{7,7},{4,20},{5,37},{6,54},{10,10},{11,... | collective-permute-start | bytes 786440 | tf_op jit(solution)/shard_map/ppermute | solution.py:170
  77.2 0.2 collective-permute-start.1
  77.4 8.7 %collective-permute-start.2 = (f32[128,512]{1,0:T(8,128)}, f32[128,512]{1,0:T(8,128)S(1)}, u32[]{:S(2)}, u32[]{:S(2)}) collective-permute-start(f32[128,512]{1,0:T(8,128)} %get-tuple-element.8), channel_id=1, source_target_pairs={{0,2},{1,19},{2,32},{3,49},{7,5},{4,22},{5,39},{6,52},{10,8},{11,2... | collective-permute-start | bytes 786440 | tf_op jit(solution)/shard_map/ppermute | solution.py:170
  86.1 5.6 %collective-permute-start.3 = (f32[128,512]{1,0:T(8,128)}, f32[128,512]{1,0:T(8,128)}, u32[]{:S(2)}, u32[]{:S(2)}) collective-permute-start(f32[128,512]{1,0:T(8,128)} %get-tuple-element.9), channel_id=1, source_target_pairs={{0,3},{1,16},{2,33},{3,50},{7,6},{4,23},{5,36},{6,53},{10,9},{11,2... | collective-permute-start | bytes 786440 | tf_op jit(solution)/shard_map/ppermute | solution.py:170
  91.7 0.0 copy-done
  91.7 4.1 %copy.8 = bf16[20000,64]{1,0:T(8,128)(2,1)} copy(bf16[20000,64]{0,1:T(8,128)(2,1)S(1)} %copy-done) | data formatting | bytes 5120000 | tf_op args[4]
  95.8 4.2 %gather_fusion = bf16[512,64]{1,0:T(8,128)(2,1)S(1)} fusion(bf16[20000,64]{1,0:T(8,128)(2,1)} %copy.8, s32[1024]{0:T(1024)S(1)} %pad_clamp_fusion), kind=kCustom, calls=%fused_computation | custom fusion | bytes 133120 | tf_op jit(solution)/shard_map/jit(_take)/gather | solution.py:178
  99.9 0.0 collective-permute-done
  99.9 0.0 collective-permute-done.1
  100.0 4.0 %collective-permute-done.2 = f32[128,512]{1,0:T(8,128)S(1)} collective-permute-done((f32[128,512]{1,0:T(8,128)}, f32[128,512]{1,0:T(8,128)S(1)}, u32[]{:S(2)}, u32[]{:S(2)}) %collective-permute-start.2) | collective-permute-done | bytes 262176 | tf_op jit(solution)/shard_map/ppermute | solution.py:170
  104.0 11.1 %collective-permute-done.3 = f32[128,512]{1,0:T(8,128)} collective-permute-done((f32[128,512]{1,0:T(8,128)}, f32[128,512]{1,0:T(8,128)}, u32[]{:S(2)}, u32[]{:S(2)}) %collective-permute-start.3) | collective-permute-done | bytes 262176 | tf_op jit(solution)/shard_map/ppermute | solution.py:170
  115.0 1.1 add_select_fusion
  116.1 0.0 copy-start.1
  116.1 1.0 convolution_bitcast_fusion
  117.1 0.0 copy-done.1
  (5 shorter events, 0.0 us)
Async XLA Ops:
  8.3 9.9 %copy-start.2 = (s32[1,512]{1,0:T(1,128)S(1)}, s32[1,512]{1,0:T(1,128)}, u32[]{:S(2)}) copy-start(s32[1,512]{1,0:T(1,128)} %param.8) | copy-start | bytes 6148
  8.3 83.4 %copy-start = (bf16[20000,64]{0,1:T(8,128)(2,1)S(1)}, bf16[20000,64]{0,1:T(8,128)(2,1)}, u32[]{:S(2)}) copy-start(bf16[20000,64]{0,1:T(8,128)(2,1)} %param.9) | copy-start | bytes 7680004
  8.3 62.4 %all-to-all-start = ((bf16[64,64,512]{2,1,0:T(8,128)(2,1)}), bf16[64,64,512]{2,1,0:T(8,128)(2,1)}, u32[]{:S(2)}, u32[]{:S(2)}) async-start(bf16[64,64,512]{2,1,0:T(8,128)(2,1)} %shard_map.69), calls=%async_computation | async-start | bytes 8388608 | tf_op jit(solution)/shard_map/all_to_all | solution.py:165
  75.6 24.4 %collective-permute-start = (f32[128,512]{1,0:T(8,128)}, f32[128,512]{1,0:T(8,128)S(1)}, u32[]{:S(2)}, u32[]{:S(2)}) collective-permute-start(f32[128,512]{1,0:T(8,128)} %get-tuple-element.6), channel_id=1, source_target_pairs={{0,0},{1,17},{2,34},{3,51},{7,7},{4,20},{5,37},{6,54},{10,10},{11,... | collective-permute-start | bytes 786440 | tf_op jit(solution)/shard_map/ppermute | solution.py:170
  77.2 22.8 %collective-permute-start.1 = (f32[128,512]{1,0:T(8,128)}, f32[128,512]{1,0:T(8,128)S(1)}, u32[]{:S(2)}, u32[]{:S(2)}) collective-permute-start(f32[128,512]{1,0:T(8,128)} %get-tuple-element.7), channel_id=1, source_target_pairs={{0,1},{1,18},{2,35},{3,48},{7,4},{4,21},{5,38},{6,55},{10,11},{11,... | collective-permute-start | bytes 786440 | tf_op jit(solution)/shard_map/ppermute | solution.py:170
  77.4 26.5 %collective-permute-start.2 = (f32[128,512]{1,0:T(8,128)}, f32[128,512]{1,0:T(8,128)S(1)}, u32[]{:S(2)}, u32[]{:S(2)}) collective-permute-start(f32[128,512]{1,0:T(8,128)} %get-tuple-element.8), channel_id=1, source_target_pairs={{0,2},{1,19},{2,32},{3,49},{7,5},{4,22},{5,39},{6,52},{10,8},{11,2... | collective-permute-start | bytes 786440 | tf_op jit(solution)/shard_map/ppermute | solution.py:170
  86.1 28.9 %collective-permute-start.3 = (f32[128,512]{1,0:T(8,128)}, f32[128,512]{1,0:T(8,128)}, u32[]{:S(2)}, u32[]{:S(2)}) collective-permute-start(f32[128,512]{1,0:T(8,128)} %get-tuple-element.9), channel_id=1, source_target_pairs={{0,3},{1,16},{2,33},{3,50},{7,6},{4,23},{5,36},{6,53},{10,9},{11,2... | collective-permute-start | bytes 786440 | tf_op jit(solution)/shard_map/ppermute | solution.py:170
  116.1 1.0 copy-start.1

commit v4 on v3

--- a/solution.py
+++ b/solution.py
@@ -12,27 +12,8 @@
 PARTS = 4
 OG = 16
 SHARES = 4
+SHIFTS = (2, 1, 3, 0)
 NONE = -1000
-
-
-def code_kernel(screen_ref, o_ref):
-    seen = jnp.zeros_like(screen_ref[0:1, :])
-    inner = lax.broadcasted_iota(jnp.int32, seen.shape, 1) % OG
-    codes = [jnp.full_like(seen, NONE) for _ in range(SLOTS)]
-    for t in range(TILES):
-        kept = screen_ref[t : t + 1, :]
-        for k in range(SLOTS):
-            here = (kept == 1) & (seen == k)
-            codes[k] = jnp.where(here, t * PART * OG + inner, codes[k])
-        seen = seen + kept
-    for k in range(SLOTS):
-        o_ref[k : k + 1, :] = codes[k]
-
-
-def slot_codes(screen):
-    return pl.pallas_call(
-        code_kernel, out_shape=jax.ShapeDtypeStruct((SLOTS, screen.shape[1]), jnp.int32)
-    )(screen)
 
 
 def holder(zh, low, g):
@@ -40,7 +21,19 @@
     return (away + 2 * (g & 1) * (1 - (away & 1)) - low) & 3
 
 
-def pack_kernel(code_ref, group_ref, x_hbm, o_hbm, x_ref, o_ref, pick_ref, in_sems, out_sems):
+def slot_codes(screen_ref, code_ref, orbital):
+    for k in range(SLOTS):
+        code_ref[k, orbital] = NONE
+    seen = 0
+    for t in range(TILES):
+        code_ref[seen, orbital] = t * PART * OG + orbital % OG
+        seen = seen + screen_ref[t, orbital]
+    code_ref[seen, orbital] = NONE
+
+
+def pack_kernel(
+    screen_ref, group_ref, x_hbm, o_hbm, x_ref, o_ref, pick_ref, code_ref, in_sems, out_sems
+):
     steps = x_hbm.shape[3] // OG
     arrivals = [
         pltpu.make_async_copy(
@@ -48,19 +41,23 @@
         )
         for s in range(steps)
     ]
+    runs = [[(zl * steps + s) * 8 for zl in range(2)] for s in range(steps)]
     leaving = [
         pltpu.make_async_copy(
-            o_ref.at[s * OG : (s + 1) * OG], o_hbm.at[s * OG : (s + 1) * OG], out_sems.at[s]
+            o_ref.at[run : run + 8], o_hbm.at[run : run + 8], out_sems.at[run // 8]
         )
         for s in range(steps)
+        for run in runs[s]
     ]
     for copy in arrivals:
         copy.start()
-    slots = [holder(i // 4, i % 4, group_ref[0]) * 4 + i % 4 for i in range(OG)]
+    slots = [holder(i // 4, i % 4, group_ref[0]) * 2 + i % 2 for i in range(OG)]
     width = TILES * PART * OG
     row = lax.broadcasted_iota(jnp.int32, (2 * PART, width), 0)
     place = lax.broadcasted_iota(jnp.int32, (2 * PART, width), 1) - OG * (row % PART)
     for s in range(steps):
+        for i in range(OG):
+            slot_codes(screen_ref, code_ref, s * OG + i)
         for i in range(OG):
             both = []
             for k in range(0, SLOTS, 2):
@@ -76,13 +73,14 @@
             for i in range(OG):
                 at = i * SLOTS * PART
                 to = h * SLOTS * PART
-                o_ref[s * OG + slots[i], to : to + SLOTS * PART, :] = got[at : at + SLOTS * PART]
-        leaving[s].start()
+                o_ref[runs[s][i % 4 // 2] + slots[i], to : to + SLOTS * PART, :] = got[at : at + SLOTS * PART]
+        for copy in leaving[2 * s : 2 * s + 2]:
+            copy.start()
     for copy in leaving:
         copy.wait()
 
 
-def pack(code, group, half_blocks):
+def pack(screen, group, half_blocks):
     rows, orbitals, width = half_blocks.shape
     tiled = half_blocks.reshape(TILES, PARTS, PART, orbitals, width)
     kept = rows // TILES * SLOTS
@@ -100,10 +98,11 @@
             pltpu.VMEM((steps, TILES, PARTS, PART, OG, width), jnp.bfloat16),
             pltpu.VMEM((orbitals, kept, width), jnp.bfloat16),
             pltpu.VMEM((OG * SLOTS * PART, TILES * PART * OG), jnp.bfloat16),
+            pltpu.SMEM((TILES + 1, orbitals), jnp.int32),
             pltpu.SemaphoreType.DMA((steps,)),
-            pltpu.SemaphoreType.DMA((steps,)),
+            pltpu.SemaphoreType.DMA((2 * steps,)),
         ],
-    )(code, group, tiled)
+    )(screen, group, tiled)
 
 
 def gram_kernel(first_ref, x_hbm, *refs):
@@ -127,8 +126,8 @@
         else:
             acc[...] += part
     share = acc.shape[0] // SHARES
-    for j in range(SHARES):
-        start = pl.multiple_of(((first_ref[0] + j) % SHARES) * share, share)
+    for j, shift in enumerate(SHIFTS):
+        start = pl.multiple_of(((first_ref[0] + shift) % SHARES) * share, share)
         outs[j][...] = acc[pl.ds(start, share), :]
 
 
@@ -161,13 +160,13 @@
 def per_device(half_blocks, screen, domain_length, domain_index, orbital_coeff):
     dom_width = half_blocks.shape[2]
     group = lax.axis_index("zh").reshape(1)
-    packed = pack(slot_codes(screen), group, half_blocks)
-    arrived = lax.all_to_all(packed, ("y", "x", "zl", "c"), split_axis=0, concat_axis=0, tiled=True)
+    packed = pack(screen, group, half_blocks)
+    arrived = lax.all_to_all(packed, ("zl", "y", "x", "c"), split_axis=0, concat_axis=0, tiled=True)
     columns = arrived.reshape(-1, dom_width)
     shares = gram(lax.axis_index("x").reshape(1), columns)
     total = None
-    for j, share in enumerate(shares):
-        got = lax.ppermute(share, ("zh", "zl", "c", "x"), routes(j))
+    for share, shift in zip(shares, SHIFTS):
+        got = lax.ppermute(share, ("zh", "zl", "c", "x"), routes(shift))
         total = got if total is None else total + got
     row_share = dom_width // SHARES
     length = domain_length[0]

time: 117 us -> 111 us (0.949)
  the two profiles are of different devices: /device:TPU:52 before, /device:TPU:55 now
where the time goes in v4:
time: 111 us; the launch traced here: 110 us
  waiting for transfers between devices  59 us (53%)
  starting transfers between devices  28.1 us (25%)
  Pallas kernels  11.3 us (10%)
  local copies, waits for them, and re-layouts  8.28 us (7%)
  between operations  1.43 us (1%)
    all_to_all x1, waiting for transfers between devices, per_device(): lax.all_to_all(packed, ('zl', 'y', 'x', 'c'), split_axis=0, concat_axis=0...  49 us
    ppermute x4, starting transfers between devices, per_device(): got = lax.ppermute(share, ('zh', 'zl', 'c', 'x'), routes(shift))  18.6 us
    ppermute x4, waiting for transfers between devices, per_device(): got = lax.ppermute(share, ('zh', 'zl', 'c', 'x'), routes(shift))  10 us
    all_to_all x1, starting transfers between devices, per_device(): lax.all_to_all(packed, ('zl', 'y', 'x', 'c'), split_axis=0, concat_axis=0...  9.51 us
    pallas_call x1, Pallas kernels, pack(): pl.pallas_call(pack_kernel, in_specs=[pl.BlockSpec(memory_space=pltpu.SME...  6.5 us
    pallas_call x1, Pallas kernels, gram(): pl.pallas_call(gram_kernel, in_specs=[pl.BlockSpec(memory_space=pltpu.SME...  4.84 us
    gather x1, local copies, waits for them, and re-layouts, per_device(): jnp.take(orbital_coeff, domain_index[0], axis=0).astype(jnp.float32)  4.16 us
    unnamed x7, local copies, waits for them, and re-layouts  4.11 us
  transfers between devices with their start and end apart: 5, of which 3 were waited for; matrix products, arithmetic and copies ran while one was open for 8% of the time, Pallas kernels for 0%

profile of v4, /device:TPU:55, one launch (start us, length us, event | category | flops | bytes accessed | tf_op | source)
XLA Modules:
  0.0 110.2 jit_solution(9950642480758772564)
XLA Ops:
  0.6 6.5 %shard_map.68 = bf16[64,64,512]{2,1,0:T(8,128)(2,1)} custom-call(s32[8,64]{1,0:T(8,128)} %screen_ref.1, s32[1]{0:T(128)} %bitcast.2.group_ref, bf16[8,4,4,64,512]{4,3,2,1,0:T(8,128)(2,1)} %bitcast.15), custom_call_target="tpu_custom_call" | custom-call | tf_op jit(solution)/shard_map/pallas_call | solution.py:88
  7.1 0.0 copy-start.2
  7.2 0.0 copy-start
  7.2 9.5 %all-to-all-start = ((bf16[64,64,512]{2,1,0:T(8,128)(2,1)}), bf16[64,64,512]{2,1,0:T(8,128)(2,1)}, u32[]{:S(2)}, u32[]{:S(2)}) async-start(bf16[64,64,512]{2,1,0:T(8,128)(2,1)} %shard_map.68), calls=%async_computation | async-start | bytes 8388608 | tf_op jit(solution)/shard_map/all_to_all | solution.py:164
  17.3 0.0 copy-done.2
  17.4 49.0 %all-to-all-done = bf16[64,64,512]{2,1,0:T(8,128)(2,1)} async-done(((bf16[64,64,512]{2,1,0:T(8,128)(2,1)}), bf16[64,64,512]{2,1,0:T(8,128)(2,1)}, u32[]{:S(2)}, u32[]{:S(2)}) %all-to-all-start) | async-done | bytes 4194336 | tf_op jit(solution)/shard_map/all_to_all | solution.py:164
  66.3 4.8 %shard_map.69 = (f32[128,512]{1,0:T(8,128)}, f32[128,512]{1,0:T(8,128)}, f32[128,512]{1,0:T(8,128)}, f32[128,512]{1,0:T(8,128)}) custom-call(s32[1]{0:T(128)} %bitcast.1.first_ref, bf16[4096,512]{1,0:T(8,128)(2,1)} %bitcast.4.x_hbm), custom_call_target="tpu_custom_call" | custom-call | tf_op jit(solution)/shard_map/pallas_call | solution.py:137
  71.2 8.8 %collective-permute-start = (f32[128,512]{1,0:T(8,128)}, f32[128,512]{1,0:T(8,128)S(1)}, u32[]{:S(2)}, u32[]{:S(2)}) collective-permute-start(f32[128,512]{1,0:T(8,128)} %get-tuple-element.6), channel_id=1, source_target_pairs={{0,2},{1,19},{2,32},{3,49},{7,5},{4,22},{5,39},{6,52},{10,8},{11,2... | collective-permute-start | bytes 786440 | tf_op jit(solution)/shard_map/ppermute | solution.py:169
  80.0 3.7 %collective-permute-start.1 = (f32[128,512]{1,0:T(8,128)}, f32[128,512]{1,0:T(8,128)S(1)}, u32[]{:S(2)}, u32[]{:S(2)}) collective-permute-start(f32[128,512]{1,0:T(8,128)} %get-tuple-element.7), channel_id=1, source_target_pairs={{0,1},{1,18},{2,35},{3,48},{7,4},{4,21},{5,38},{6,55},{10,11},{11,... | collective-permute-start | bytes 786440 | tf_op jit(solution)/shard_map/ppermute | solution.py:169
  83.7 0.0 collective-permute-start.2
  83.7 6.1 %collective-permute-start.3 = (f32[128,512]{1,0:T(8,128)}, f32[128,512]{1,0:T(8,128)}, u32[]{:S(2)}, u32[]{:S(2)}) collective-permute-start(f32[128,512]{1,0:T(8,128)} %get-tuple-element.9), channel_id=1, source_target_pairs={{0,0},{1,17},{2,34},{3,51},{7,7},{4,20},{5,37},{6,54},{10,10},{11,... | collective-permute-start | bytes 786440 | tf_op jit(solution)/shard_map/ppermute | solution.py:169
  89.8 0.0 copy-done
  89.8 4.1 %copy.8 = bf16[20000,64]{1,0:T(8,128)(2,1)} copy(bf16[20000,64]{0,1:T(8,128)(2,1)S(1)} %copy-done) | data formatting | bytes 5120000 | tf_op args[4]
  93.9 4.2 %gather_fusion = bf16[512,64]{1,0:T(8,128)(2,1)S(1)} fusion(bf16[20000,64]{1,0:T(8,128)(2,1)} %copy.8, s32[1024]{0:T(1024)S(1)} %pad_clamp_fusion), kind=kCustom, calls=%fused_computation | custom fusion | bytes 133120 | tf_op jit(solution)/shard_map/jit(_take)/gather | solution.py:177
  98.1 0.0 collective-permute-done
  98.1 0.0 collective-permute-done.1
  98.1 1.6 %collective-permute-done.2 = f32[128,512]{1,0:T(8,128)S(1)} collective-permute-done((f32[128,512]{1,0:T(8,128)}, f32[128,512]{1,0:T(8,128)S(1)}, u32[]{:S(2)}, u32[]{:S(2)}) %collective-permute-start.2) | collective-permute-done | bytes 262176 | tf_op jit(solution)/shard_map/ppermute | solution.py:169
  99.7 8.4 %collective-permute-done.3 = f32[128,512]{1,0:T(8,128)} collective-permute-done((f32[128,512]{1,0:T(8,128)}, f32[128,512]{1,0:T(8,128)}, u32[]{:S(2)}, u32[]{:S(2)}) %collective-permute-start.3) | collective-permute-done | bytes 262176 | tf_op jit(solution)/shard_map/ppermute | solution.py:169
  108.1 1.1 add_select_fusion
  109.2 0.0 copy-start.1
  109.2 1.0 convolution_bitcast_fusion
  110.2 0.0 copy-done.1
  (5 shorter events, 0.0 us)
Async XLA Ops:
  7.1 10.2 %copy-start.2 = (s32[1,512]{1,0:T(1,128)S(1)}, s32[1,512]{1,0:T(1,128)}, u32[]{:S(2)}) copy-start(s32[1,512]{1,0:T(1,128)} %param.8) | copy-start | bytes 6148
  7.2 82.7 %copy-start = (bf16[20000,64]{0,1:T(8,128)(2,1)S(1)}, bf16[20000,64]{0,1:T(8,128)(2,1)}, u32[]{:S(2)}) copy-start(bf16[20000,64]{0,1:T(8,128)(2,1)} %param.9) | copy-start | bytes 7680004
  7.2 59.2 %all-to-all-start = ((bf16[64,64,512]{2,1,0:T(8,128)(2,1)}), bf16[64,64,512]{2,1,0:T(8,128)(2,1)}, u32[]{:S(2)}, u32[]{:S(2)}) async-start(bf16[64,64,512]{2,1,0:T(8,128)(2,1)} %shard_map.68), calls=%async_computation | async-start | bytes 8388608 | tf_op jit(solution)/shard_map/all_to_all | solution.py:164
  71.2 26.9 %collective-permute-start = (f32[128,512]{1,0:T(8,128)}, f32[128,512]{1,0:T(8,128)S(1)}, u32[]{:S(2)}, u32[]{:S(2)}) collective-permute-start(f32[128,512]{1,0:T(8,128)} %get-tuple-element.6), channel_id=1, source_target_pairs={{0,2},{1,19},{2,32},{3,49},{7,5},{4,22},{5,39},{6,52},{10,8},{11,2... | collective-permute-start | bytes 786440 | tf_op jit(solution)/shard_map/ppermute | solution.py:169
  80.0 18.2 %collective-permute-start.1 = (f32[128,512]{1,0:T(8,128)}, f32[128,512]{1,0:T(8,128)S(1)}, u32[]{:S(2)}, u32[]{:S(2)}) collective-permute-start(f32[128,512]{1,0:T(8,128)} %get-tuple-element.7), channel_id=1, source_target_pairs={{0,1},{1,18},{2,35},{3,48},{7,4},{4,21},{5,38},{6,55},{10,11},{11,... | collective-permute-start | bytes 786440 | tf_op jit(solution)/shard_map/ppermute | solution.py:169
  83.7 16.0 %collective-permute-start.2 = (f32[128,512]{1,0:T(8,128)}, f32[128,512]{1,0:T(8,128)S(1)}, u32[]{:S(2)}, u32[]{:S(2)}) collective-permute-start(f32[128,512]{1,0:T(8,128)} %get-tuple-element.8), channel_id=1, source_target_pairs={{0,3},{1,16},{2,33},{3,50},{7,6},{4,23},{5,36},{6,53},{10,9},{11,2... | collective-permute-start | bytes 786440 | tf_op jit(solution)/shard_map/ppermute | solution.py:169
  83.7 24.5 %collective-permute-start.3 = (f32[128,512]{1,0:T(8,128)}, f32[128,512]{1,0:T(8,128)}, u32[]{:S(2)}, u32[]{:S(2)}) collective-permute-start(f32[128,512]{1,0:T(8,128)} %get-tuple-element.9), channel_id=1, source_target_pairs={{0,0},{1,17},{2,34},{3,51},{7,7},{4,20},{5,37},{6,54},{10,10},{11,... | collective-permute-start | bytes 786440 | tf_op jit(solution)/shard_map/ppermute | solution.py:169
  109.2 1.0 copy-start.1

commit v5 on v4

--- a/solution.py
+++ b/solution.py
@@ -16,9 +16,10 @@
 NONE = -1000
 
 
-def holder(zh, low, g):
+def holder(zh, zl, c, g):
     away = (zh - g) & 3
-    return (away + 2 * (g & 1) * (1 - (away & 1)) - low) & 3
+    turn = (away + 1) & 3 if zl else away ^ 1
+    return (1 - (away >> 1) if zl else (away ^ (away >> 1)) & 1), (turn - 2 * c) & 3
 
 
 def slot_codes(screen_ref, code_ref, orbital):
@@ -51,7 +52,10 @@
     ]
     for copy in arrivals:
         copy.start()
-    slots = [holder(i // 4, i % 4, group_ref[0]) * 2 + i % 2 for i in range(OG)]
+    slots = []
+    for i in range(OG):
+        pair, x = holder(i // 4, i // 2 % 2, i % 2, group_ref[0])
+        slots.append(pair * steps * 8 + x * 2 + i % 2)
     width = TILES * PART * OG
     row = lax.broadcasted_iota(jnp.int32, (2 * PART, width), 0)
     place = lax.broadcasted_iota(jnp.int32, (2 * PART, width), 1) - OG * (row % PART)
@@ -73,7 +77,7 @@
             for i in range(OG):
                 at = i * SLOTS * PART
                 to = h * SLOTS * PART
-                o_ref[runs[s][i % 4 // 2] + slots[i], to : to + SLOTS * PART, :] = got[at : at + SLOTS * PART]
+                o_ref[s * 8 + slots[i], to : to + SLOTS * PART, :] = got[at : at + SLOTS * PART]
         for copy in leaving[2 * s : 2 * s + 2]:
             copy.start()
     for copy in leaving:
@@ -105,33 +109,39 @@
     )(screen, group, tiled)
 
 
-def gram_kernel(first_ref, x_hbm, *refs):
-    outs, x_ref, acc, sems = refs[:SHARES], refs[-3], refs[-2], refs[-1]
+def gram_kernel(place_ref, x_hbm, *refs):
+    outs, x_ref, sems = refs[:SHARES], refs[-2], refs[-1]
     parts = sems.shape[0]
     depth = x_hbm.shape[0] // parts
+    share = x_hbm.shape[1] // SHARES
+    spans = [slice(p * depth, (p + 1) * depth) for p in range(parts)]
     arrivals = [
-        pltpu.make_async_copy(
-            x_hbm.at[p * depth : (p + 1) * depth], x_ref.at[p * depth : (p + 1) * depth], sems.at[p]
-        )
-        for p in range(parts)
+        pltpu.make_async_copy(x_hbm.at[span], x_ref.at[span], sems.at[p])
+        for p, span in enumerate(spans)
     ]
     for copy in arrivals:
         copy.start()
-    for p in range(parts):
+    for p, span in enumerate(spans):
         arrivals[p].wait()
-        x = x_ref[p * depth : (p + 1) * depth, :]
-        part = lax.dot_general(x, x, (((0,), (0,)), ((), ())), preferred_element_type=jnp.float32)
-        if p == 0:
-            acc[...] = part
-        else:
-            acc[...] += part
-    share = acc.shape[0] // SHARES
-    for j, shift in enumerate(SHIFTS):
-        start = pl.multiple_of(((first_ref[0] + shift) % SHARES) * share, share)
-        outs[j][...] = acc[pl.ds(start, share), :]
-
-
-def gram(first, columns, parts=4):
+        left = []
+        for shift in SHIFTS:
+            start = pl.multiple_of((place_ref[0] ^ shift) * share, share)
+            left.append(x_ref[span, pl.ds(start, share)])
+        part = lax.dot_general(
+            jnp.concatenate(left, axis=1),
+            x_ref[span, :],
+            (((0,), (0,)), ((), ())),
+            preferred_element_type=jnp.float32,
+        )
+        for j in range(SHARES):
+            piece = part[j * share : (j + 1) * share]
+            if p == 0:
+                outs[j][...] = piece
+            else:
+                outs[j][...] += piece
+
+
+def gram(place, columns, parts=4):
     rows, width = columns.shape
     share = width // SHARES
     return pl.pallas_call(
@@ -141,19 +151,20 @@
         out_shape=[jax.ShapeDtypeStruct((share, width), jnp.float32)] * SHARES,
         scratch_shapes=[
             pltpu.VMEM((rows, width), jnp.bfloat16),
-            pltpu.VMEM((width, width), jnp.float32),
             pltpu.SemaphoreType.DMA((parts,)),
         ],
-    )(first, columns)
-
-
-def routes(j):
+    )(place, columns)
+
+
+def routes(shift):
     pairs = []
     for g in range(4):
-        for low in range(4):
-            for owner in range(4):
-                x = holder(owner, low, g)
-                pairs.append(((g * 4 + low) * 4 + x, (owner * 4 + low) * 4 + (x + j) % 4))
+        for zh in range(4):
+            for zl in range(2):
+                for c in range(2):
+                    pair, x = holder(zh, zl, c, g)
+                    source = ((g * 2 + pair) * 2 + c) * 4 + x
+                    pairs.append((source, ((zh * 2 + zl) * 2 + c) * 4 + (x ^ shift)))
     return pairs
 
 

time: 111 us -> 111 us (level)
  the two profiles are of different devices: /device:TPU:55 before, /device:TPU:3 now
where the time goes in v5:
time: 111 us
  waiting for transfers between devices  61.6 us (55%)
  starting transfers between devices  26 us (23%)
  Pallas kernels  11.3 us (10%)
  local copies, waits for them, and re-layouts  8.27 us (7%)
  between operations  1.43 us (1%)
    all_to_all x1, waiting for transfers between devices, per_device(): lax.all_to_all(packed, ('zl', 'y', 'x', 'c'), split_axis=0, concat_axis=0...  51.9 us
    ppermute x4, starting transfers between devices, per_device(): got = lax.ppermute(share, ('zh', 'zl', 'c', 'x'), routes(shift))  16.1 us
    all_to_all x1, starting transfers between devices, per_device(): lax.all_to_all(packed, ('zl', 'y', 'x', 'c'), split_axis=0, concat_axis=0...  9.99 us
    ppermute x4, waiting for transfers between devices, per_device(): got = lax.ppermute(share, ('zh', 'zl', 'c', 'x'), routes(shift))  9.7 us
    pallas_call x1, Pallas kernels, pack(): pl.pallas_call(pack_kernel, in_specs=[pl.BlockSpec(memory_space=pltpu.SME...  6.49 us
    pallas_call x1, Pallas kernels, gram(): pl.pallas_call(gram_kernel, in_specs=[pl.BlockSpec(memory_space=pltpu.SME...  4.76 us
    gather x1, local copies, waits for them, and re-layouts, per_device(): jnp.take(orbital_coeff, domain_index[0], axis=0).astype(jnp.float32)  4.16 us
    unnamed x7, local copies, waits for them, and re-layouts  4.11 us
  transfers between devices with their start and end apart: 5, of which 3 were waited for; matrix products, arithmetic and copies ran while one was open for 7% of the time, Pallas kernels for 0%

profile of v5, /device:TPU:3, one launch (start us, length us, event | category | flops | bytes accessed | tf_op | source)
XLA Modules:
  0.0 110.6 jit_solution(8147679747136610287)
XLA Ops:
  0.6 6.5 %shard_map.68 = bf16[64,64,512]{2,1,0:T(8,128)(2,1)} custom-call(s32[8,64]{1,0:T(8,128)} %screen_ref.1, s32[1]{0:T(128)} %bitcast.2.group_ref, bf16[8,4,4,64,512]{4,3,2,1,0:T(8,128)(2,1)} %bitcast.15), custom_call_target="tpu_custom_call" | custom-call | tf_op jit(solution)/shard_map/pallas_call | solution.py:92
  7.1 0.0 copy-start.2
  7.1 0.0 copy-start
  7.2 10.0 %all-to-all-start = ((bf16[64,64,512]{2,1,0:T(8,128)(2,1)}), bf16[64,64,512]{2,1,0:T(8,128)(2,1)}, u32[]{:S(2)}, u32[]{:S(2)}) async-start(bf16[64,64,512]{2,1,0:T(8,128)(2,1)} %shard_map.68), calls=%async_computation | async-start | bytes 8388608 | tf_op jit(solution)/shard_map/all_to_all | solution.py:175
  17.8 0.0 copy-done.2
  17.9 51.9 %all-to-all-done = bf16[64,64,512]{2,1,0:T(8,128)(2,1)} async-done(((bf16[64,64,512]{2,1,0:T(8,128)(2,1)}), bf16[64,64,512]{2,1,0:T(8,128)(2,1)}, u32[]{:S(2)}, u32[]{:S(2)}) %all-to-all-start) | async-done | bytes 4194336 | tf_op jit(solution)/shard_map/all_to_all | solution.py:175
  69.7 4.8 %shard_map.69 = (f32[128,512]{1,0:T(8,128)}, f32[128,512]{1,0:T(8,128)}, f32[128,512]{1,0:T(8,128)}, f32[128,512]{1,0:T(8,128)}) custom-call(s32[1]{0:T(128)} %bitcast.1.place_ref, bf16[4096,512]{1,0:T(8,128)(2,1)} %bitcast.4.x_hbm), custom_call_target="tpu_custom_call" | custom-call | tf_op jit(solution)/shard_map/pallas_call | solution.py:147
  74.5 9.0 %collective-permute-start = (f32[128,512]{1,0:T(8,128)}, f32[128,512]{1,0:T(8,128)S(1)}, u32[]{:S(2)}, u32[]{:S(2)}) collective-permute-start(f32[128,512]{1,0:T(8,128)} %get-tuple-element.6), channel_id=1, source_target_pairs={{1,3},{7,5},{9,11},{15,13},{8,18},{14,20},{10,24},{12,30},{11,33},... | collective-permute-start | bytes 786440 | tf_op jit(solution)/shard_map/ppermute | solution.py:180
  83.5 0.2 collective-permute-start.1
  83.7 0.8 collective-permute-start.2
  84.5 6.0 %collective-permute-start.3 = (f32[128,512]{1,0:T(8,128)}, f32[128,512]{1,0:T(8,128)}, u32[]{:S(2)}, u32[]{:S(2)}) collective-permute-start(f32[128,512]{1,0:T(8,128)} %get-tuple-element.9), channel_id=1, source_target_pairs={{1,1},{7,7},{9,9},{15,15},{8,16},{14,22},{10,26},{12,28},{11,35},{... | collective-permute-start | bytes 786440 | tf_op jit(solution)/shard_map/ppermute | solution.py:180
  90.6 0.0 copy-done
  90.6 4.1 %copy.8 = bf16[20000,64]{1,0:T(8,128)(2,1)} copy(bf16[20000,64]{0,1:T(8,128)(2,1)S(1)} %copy-done) | data formatting | bytes 5120000 | tf_op args[4]
  94.7 4.2 %gather_fusion = bf16[512,64]{1,0:T(8,128)(2,1)S(1)} fusion(bf16[20000,64]{1,0:T(8,128)(2,1)} %copy.8, s32[1024]{0:T(1024)S(1)} %pad_clamp_fusion), kind=kCustom, calls=%fused_computation | custom fusion | bytes 133120 | tf_op jit(solution)/shard_map/jit(_take)/gather | solution.py:188
  98.8 0.0 collective-permute-done
  98.9 0.0 collective-permute-done.1
  98.9 5.2 %collective-permute-done.2 = f32[128,512]{1,0:T(8,128)S(1)} collective-permute-done((f32[128,512]{1,0:T(8,128)}, f32[128,512]{1,0:T(8,128)S(1)}, u32[]{:S(2)}, u32[]{:S(2)}) %collective-permute-start.2) | collective-permute-done | bytes 262176 | tf_op jit(solution)/shard_map/ppermute | solution.py:180
  104.0 4.5 %collective-permute-done.3 = f32[128,512]{1,0:T(8,128)} collective-permute-done((f32[128,512]{1,0:T(8,128)}, f32[128,512]{1,0:T(8,128)}, u32[]{:S(2)}, u32[]{:S(2)}) %collective-permute-start.3) | collective-permute-done | bytes 262176 | tf_op jit(solution)/shard_map/ppermute | solution.py:180
  108.6 1.1 add_select_fusion
  109.6 0.0 copy-start.1
  109.6 1.0 convolution_bitcast_fusion
  110.6 0.0 copy-done.1
  (5 shorter events, 0.0 us)
Async XLA Ops:
  7.1 10.7 %copy-start.2 = (s32[1,512]{1,0:T(1,128)S(1)}, s32[1,512]{1,0:T(1,128)}, u32[]{:S(2)}) copy-start(s32[1,512]{1,0:T(1,128)} %param.8) | copy-start | bytes 6148
  7.1 83.4 %copy-start = (bf16[20000,64]{0,1:T(8,128)(2,1)S(1)}, bf16[20000,64]{0,1:T(8,128)(2,1)}, u32[]{:S(2)}) copy-start(bf16[20000,64]{0,1:T(8,128)(2,1)} %param.9) | copy-start | bytes 7680004
  7.2 62.6 %all-to-all-start = ((bf16[64,64,512]{2,1,0:T(8,128)(2,1)}), bf16[64,64,512]{2,1,0:T(8,128)(2,1)}, u32[]{:S(2)}, u32[]{:S(2)}) async-start(bf16[64,64,512]{2,1,0:T(8,128)(2,1)} %shard_map.68), calls=%async_computation | async-start | bytes 8388608 | tf_op jit(solution)/shard_map/all_to_all | solution.py:175
  74.5 24.4 %collective-permute-start = (f32[128,512]{1,0:T(8,128)}, f32[128,512]{1,0:T(8,128)S(1)}, u32[]{:S(2)}, u32[]{:S(2)}) collective-permute-start(f32[128,512]{1,0:T(8,128)} %get-tuple-element.6), channel_id=1, source_target_pairs={{1,3},{7,5},{9,11},{15,13},{8,18},{14,20},{10,24},{12,30},{11,33},... | collective-permute-start | bytes 786440 | tf_op jit(solution)/shard_map/ppermute | solution.py:180
  83.5 15.3 %collective-permute-start.1 = (f32[128,512]{1,0:T(8,128)}, f32[128,512]{1,0:T(8,128)S(1)}, u32[]{:S(2)}, u32[]{:S(2)}) collective-permute-start(f32[128,512]{1,0:T(8,128)} %get-tuple-element.7), channel_id=1, source_target_pairs={{1,0},{7,6},{9,8},{15,14},{8,17},{14,23},{10,27},{12,29},{11,34},{... | collective-permute-start | bytes 786440 | tf_op jit(solution)/shard_map/ppermute | solution.py:180
  83.7 20.3 %collective-permute-start.2 = (f32[128,512]{1,0:T(8,128)}, f32[128,512]{1,0:T(8,128)S(1)}, u32[]{:S(2)}, u32[]{:S(2)}) collective-permute-start(f32[128,512]{1,0:T(8,128)} %get-tuple-element.8), channel_id=1, source_target_pairs={{1,2},{7,4},{9,10},{15,12},{8,19},{14,21},{10,25},{12,31},{11,32},... | collective-permute-start | bytes 786440 | tf_op jit(solution)/shard_map/ppermute | solution.py:180
  84.5 24.0 %collective-permute-start.3 = (f32[128,512]{1,0:T(8,128)}, f32[128,512]{1,0:T(8,128)}, u32[]{:S(2)}, u32[]{:S(2)}) collective-permute-start(f32[128,512]{1,0:T(8,128)} %get-tuple-element.9), channel_id=1, source_target_pairs={{1,1},{7,7},{9,9},{15,15},{8,16},{14,22},{10,26},{12,28},{11,35},{... | collective-permute-start | bytes 786440 | tf_op jit(solution)/shard_map/ppermute | solution.py:180
  109.6 1.0 copy-start.1

commit v6 on v5

--- a/solution.py
+++ b/solution.py
@@ -153,6 +153,7 @@
             pltpu.VMEM((rows, width), jnp.bfloat16),
             pltpu.SemaphoreType.DMA((parts,)),
         ],
+        compiler_params=pltpu.CompilerParams(vmem_limit_bytes=12 << 20),
     )(place, columns)
 
 

time: 111 us -> 109 us (0.982)
  waiting for transfers between devices: 61.6 us -> 59.5 us
  local copies, waits for them, and re-layouts: 8.27 us -> 10 us
    ppermute x4, waiting for transfers between devices: 9.7 us -> 7.66 us  [per_device(): got = lax.ppermute(share, ('zh', 'zl', 'c', 'x'), routes(shift))]
    unnamed x7 -> x5, local copies, waits for them, and re-layouts: 4.11 us -> 5.86 us
  transfers between devices with their start and end apart: 5 -> 5, of which waited for: 3 -> 3; matrix products, arithmetic and copies ran while one was open for 7% -> 9% of each run, Pallas kernels for 0% -> 0%
where the time goes in v6:
time: 109 us; the launch traced here: 108 us
  waiting for transfers between devices  59.5 us (55%)
  starting transfers between devices  25.9 us (24%)
  Pallas kernels  10.4 us (10%)
  local copies, waits for them, and re-layouts  10 us (9%)
  between operations  1.41 us (1%)
    all_to_all x1, waiting for transfers between devices, per_device(): lax.all_to_all(packed, ('zl', 'y', 'x', 'c'), split_axis=0, concat_axis=0...  51.9 us
    ppermute x4, starting transfers between devices, per_device(): got = lax.ppermute(share, ('zh', 'zl', 'c', 'x'), routes(shift))  16.1 us
    all_to_all x1, starting transfers between devices, per_device(): lax.all_to_all(packed, ('zl', 'y', 'x', 'c'), split_axis=0, concat_axis=0...  9.86 us
    ppermute x4, waiting for transfers between devices, per_device(): got = lax.ppermute(share, ('zh', 'zl', 'c', 'x'), routes(shift))  7.66 us
    pallas_call x1, Pallas kernels, pack(): pl.pallas_call(pack_kernel, in_specs=[pl.BlockSpec(memory_space=pltpu.SME...  6.48 us
    unnamed x5, local copies, waits for them, and re-layouts  5.86 us
    gather x1, local copies, waits for them, and re-layouts, per_device(): jnp.take(orbital_coeff, domain_index[0], axis=0).astype(jnp.float32)  4.16 us
    pallas_call x1, Pallas kernels, gram(): pl.pallas_call(gram_kernel, in_specs=[pl.BlockSpec(memory_space=pltpu.SME...  3.89 us
  transfers between devices with their start and end apart: 5, of which 3 were waited for; matrix products, arithmetic and copies ran while one was open for 9% of the time, Pallas kernels for 0%

profile of v6, /device:TPU:3, one launch (start us, length us, event | category | flops | bytes accessed | tf_op | source)
XLA Modules:
  0.0 108.4 jit_solution(16512257817040145089)
XLA Ops:
  0.6 6.5 %shard_map.68 = bf16[64,64,512]{2,1,0:T(8,128)(2,1)} custom-call(s32[8,64]{1,0:T(8,128)} %screen_ref.1, s32[1]{0:T(128)} %bitcast.2.group_ref, bf16[8,4,4,64,512]{4,3,2,1,0:T(8,128)(2,1)} %bitcast.15), custom_call_target="tpu_custom_call" | custom-call | tf_op jit(solution)/shard_map/pallas_call | solution.py:92
  7.1 0.0 copy-start.1
  7.1 9.9 %all-to-all-start = ((bf16[64,64,512]{2,1,0:T(8,128)(2,1)}), bf16[64,64,512]{2,1,0:T(8,128)(2,1)}, u32[]{:S(2)}, u32[]{:S(2)}) async-start(bf16[64,64,512]{2,1,0:T(8,128)(2,1)} %shard_map.68), calls=%async_computation | async-start | bytes 8388608 | tf_op jit(solution)/shard_map/all_to_all | solution.py:176
  17.7 0.0 copy-done.1
  17.7 51.9 %all-to-all-done = bf16[64,64,512]{2,1,0:T(8,128)(2,1)} async-done(((bf16[64,64,512]{2,1,0:T(8,128)(2,1)}), bf16[64,64,512]{2,1,0:T(8,128)(2,1)}, u32[]{:S(2)}, u32[]{:S(2)}) %all-to-all-start) | async-done | bytes 4194336 | tf_op jit(solution)/shard_map/all_to_all | solution.py:176
  69.6 3.9 %shard_map.69 = (f32[128,512]{1,0:T(8,128)S(1)}, f32[128,512]{1,0:T(8,128)S(1)}, f32[128,512]{1,0:T(8,128)S(1)}, f32[128,512]{1,0:T(8,128)S(1)}) custom-call(s32[1]{0:T(128)} %bitcast.1.place_ref, bf16[4096,512]{1,0:T(8,128)(2,1)} %bitcast.4.x_hbm), custom_call_target="tpu_custom_call" | custom-call | tf_op jit(solution)/shard_map/pallas_call | solution.py:147
  73.5 9.0 %collective-permute-start = (f32[128,512]{1,0:T(8,128)S(1)}, f32[128,512]{1,0:T(8,128)S(1)}, u32[]{:S(2)}, u32[]{:S(2)}) collective-permute-start(f32[128,512]{1,0:T(8,128)S(1)} %get-tuple-element.6), channel_id=1, source_target_pairs={{1,3},{7,5},{9,11},{15,13},{8,18},{14,20},{10,24},{12,30},{11,33},... | collective-permute-start | bytes 786440 | tf_op jit(solution)/shard_map/ppermute | solution.py:181
  82.5 0.2 collective-permute-start.1
  82.7 0.8 collective-permute-start.2
  83.5 6.0 %collective-permute-start.3 = (f32[128,512]{1,0:T(8,128)S(1)}, f32[128,512]{1,0:T(8,128)S(1)}, u32[]{:S(2)}, u32[]{:S(2)}) collective-permute-start(f32[128,512]{1,0:T(8,128)S(1)} %get-tuple-element.9), channel_id=1, source_target_pairs={{1,1},{7,7},{9,9},{15,15},{8,16},{14,22},{10,26},{12,28},{11,35},{... | collective-permute-start | bytes 786440 | tf_op jit(solution)/shard_map/ppermute | solution.py:181
  89.5 5.8 %copy.8 = bf16[20000,64]{1,0:T(8,128)(2,1)} copy(bf16[20000,64]{0,1:T(8,128)(2,1)} %param.9) | data formatting | bytes 5120000 | tf_op args[4]
  95.4 4.2 %gather_fusion = bf16[512,64]{1,0:T(8,128)(2,1)S(1)} fusion(bf16[20000,64]{1,0:T(8,128)(2,1)} %copy.8, s32[1024]{0:T(1024)S(1)} %pad_clamp_fusion), kind=kCustom, calls=%fused_computation | custom fusion | bytes 133120 | tf_op jit(solution)/shard_map/jit(_take)/gather | solution.py:189
  99.6 0.0 collective-permute-done
  99.6 0.0 collective-permute-done.1
  99.6 3.0 %collective-permute-done.2 = f32[128,512]{1,0:T(8,128)S(1)} collective-permute-done((f32[128,512]{1,0:T(8,128)S(1)}, f32[128,512]{1,0:T(8,128)S(1)}, u32[]{:S(2)}, u32[]{:S(2)}) %collective-permute-start.2) | collective-permute-done | bytes 262176 | tf_op jit(solution)/shard_map/ppermute | solution.py:181
  102.6 4.6 %collective-permute-done.3 = f32[128,512]{1,0:T(8,128)S(1)} collective-permute-done((f32[128,512]{1,0:T(8,128)S(1)}, f32[128,512]{1,0:T(8,128)S(1)}, u32[]{:S(2)}, u32[]{:S(2)}) %collective-permute-start.3) | collective-permute-done | bytes 262176 | tf_op jit(solution)/shard_map/ppermute | solution.py:181
  107.2 0.1 add_select_fusion
  107.3 0.0 copy-start
  107.4 1.0 convolution_bitcast_fusion
  108.4 0.0 copy-done
  (5 shorter events, 0.0 us)
Async XLA Ops:
  7.1 10.5 %copy-start.1 = (s32[1,512]{1,0:T(1,128)S(1)}, s32[1,512]{1,0:T(1,128)}, u32[]{:S(2)}) copy-start(s32[1,512]{1,0:T(1,128)} %param.8) | copy-start | bytes 6148
  7.1 62.4 %all-to-all-start = ((bf16[64,64,512]{2,1,0:T(8,128)(2,1)}), bf16[64,64,512]{2,1,0:T(8,128)(2,1)}, u32[]{:S(2)}, u32[]{:S(2)}) async-start(bf16[64,64,512]{2,1,0:T(8,128)(2,1)} %shard_map.68), calls=%async_computation | async-start | bytes 8388608 | tf_op jit(solution)/shard_map/all_to_all | solution.py:176
  73.5 26.1 %collective-permute-start = (f32[128,512]{1,0:T(8,128)S(1)}, f32[128,512]{1,0:T(8,128)S(1)}, u32[]{:S(2)}, u32[]{:S(2)}) collective-permute-start(f32[128,512]{1,0:T(8,128)S(1)} %get-tuple-element.6), channel_id=1, source_target_pairs={{1,3},{7,5},{9,11},{15,13},{8,18},{14,20},{10,24},{12,30},{11,33},... | collective-permute-start | bytes 786440 | tf_op jit(solution)/shard_map/ppermute | solution.py:181
  82.5 17.1 %collective-permute-start.1 = (f32[128,512]{1,0:T(8,128)S(1)}, f32[128,512]{1,0:T(8,128)S(1)}, u32[]{:S(2)}, u32[]{:S(2)}) collective-permute-start(f32[128,512]{1,0:T(8,128)S(1)} %get-tuple-element.7), channel_id=1, source_target_pairs={{1,0},{7,6},{9,8},{15,14},{8,17},{14,23},{10,27},{12,29},{11,34},{... | collective-permute-start | bytes 786440 | tf_op jit(solution)/shard_map/ppermute | solution.py:181
  82.7 19.9 %collective-permute-start.2 = (f32[128,512]{1,0:T(8,128)S(1)}, f32[128,512]{1,0:T(8,128)S(1)}, u32[]{:S(2)}, u32[]{:S(2)}) collective-permute-start(f32[128,512]{1,0:T(8,128)S(1)} %get-tuple-element.8), channel_id=1, source_target_pairs={{1,2},{7,4},{9,10},{15,12},{8,19},{14,21},{10,25},{12,31},{11,32},... | collective-permute-start | bytes 786440 | tf_op jit(solution)/shard_map/ppermute | solution.py:181
  83.5 23.7 %collective-permute-start.3 = (f32[128,512]{1,0:T(8,128)S(1)}, f32[128,512]{1,0:T(8,128)S(1)}, u32[]{:S(2)}, u32[]{:S(2)}) collective-permute-start(f32[128,512]{1,0:T(8,128)S(1)} %get-tuple-element.9), channel_id=1, source_target_pairs={{1,1},{7,7},{9,9},{15,15},{8,16},{14,22},{10,26},{12,28},{11,35},{... | collective-permute-start | bytes 786440 | tf_op jit(solution)/shard_map/ppermute | solution.py:181
  107.3 1.0 copy-start

commit v7 on v6

--- a/solution.py
+++ b/solution.py
@@ -174,6 +174,8 @@
     group = lax.axis_index("zh").reshape(1)
     packed = pack(screen, group, half_blocks)
     arrived = lax.all_to_all(packed, ("zl", "y", "x", "c"), split_axis=0, concat_axis=0, tiled=True)
+    local_coeff = jnp.take(orbital_coeff, domain_index[0], axis=0)
+    arrived, local_coeff = lax.optimization_barrier((arrived, local_coeff))
     columns = arrived.reshape(-1, dom_width)
     shares = gram(lax.axis_index("x").reshape(1), columns)
     total = None
@@ -186,7 +188,7 @@
     col_place = lax.iota(jnp.int32, dom_width)
     inside = ((row_place < length)[:, None] & (col_place < length)[None, :]).astype(jnp.float32)
     exch_rows = total * inside
-    local_coeff = jnp.take(orbital_coeff, domain_index[0], axis=0).astype(jnp.float32)
+    local_coeff = local_coeff.astype(jnp.float32)
     occ_rows = jnp.einsum("ab,bj->ja", exch_rows, local_coeff, precision=lax.Precision.HIGHEST)
     return (exch_rows[None], occ_rows[None])
 

time: 109 us -> 109 us (level)
  local copies, waits for them, and re-layouts: 10 us -> 8.42 us
  waiting for transfers between devices: 59.5 us -> 61 us
    ppermute x4, waiting for transfers between devices: 7.66 us -> 17 us  [per_device(): got = lax.ppermute(share, ('zh', 'zl', 'c', 'x'), routes(shift))]
    all_to_all x1, waiting for transfers between devices: 51.9 us -> 44 us  [per_device(): lax.all_to_all(packed, ('zl', 'y', 'x', 'c'), split_axis=0, concat_axis=0...]
    unnamed x5 -> x7, local copies, waits for them, and re-layouts: 5.86 us -> 4.26 us
  transfers between devices with their start and end apart: 5 -> 5, of which waited for: 3 -> 4; matrix products, arithmetic and copies ran while one was open for 9% -> 8% of each run, Pallas kernels for 0% -> 0%
where the time goes in v7:
time: 109 us; the launch traced here: 108 us
  waiting for transfers between devices  61 us (56%)
  starting transfers between devices  26 us (24%)
  Pallas kernels  10.4 us (10%)
  local copies, waits for them, and re-layouts  8.42 us (8%)
  between operations  1.4 us (1%)
    all_to_all x1, waiting for transfers between devices, per_device(): lax.all_to_all(packed, ('zl', 'y', 'x', 'c'), split_axis=0, concat_axis=0...  44 us
    ppermute x4, waiting for transfers between devices, per_device(): got = lax.ppermute(share, ('zh', 'zl', 'c', 'x'), routes(shift))  17 us
    ppermute x4, starting transfers between devices, per_device(): got = lax.ppermute(share, ('zh', 'zl', 'c', 'x'), routes(shift))  16.1 us
    all_to_all x1, starting transfers between devices, per_device(): lax.all_to_all(packed, ('zl', 'y', 'x', 'c'), split_axis=0, concat_axis=0...  9.99 us
    pallas_call x1, Pallas kernels, pack(): pl.pallas_call(pack_kernel, in_specs=[pl.BlockSpec(memory_space=pltpu.SME...  6.49 us
    unnamed x7, local copies, waits for them, and re-layouts  4.26 us
    gather x1, local copies, waits for them, and re-layouts, per_device(): local_coeff = jnp.take(orbital_coeff, domain_index[0], axis=0)  4.16 us
    pallas_call x1, Pallas kernels, gram(): pl.pallas_call(gram_kernel, in_specs=[pl.BlockSpec(memory_space=pltpu.SME...  3.89 us
  transfers between devices with their start and end apart: 5, of which 4 were waited for; matrix products, arithmetic and copies ran while one was open for 8% of the time, Pallas kernels for 0%

profile of v7, /device:TPU:3, one launch (start us, length us, event | category | flops | bytes accessed | tf_op | source)
XLA Modules:
  0.0 108.4 jit_solution(17860892833658229000)
XLA Ops:
  0.6 6.5 %shard_map.68 = bf16[64,64,512]{2,1,0:T(8,128)(2,1)} custom-call(s32[8,64]{1,0:T(8,128)} %screen_ref.1, s32[1]{0:T(128)} %bitcast.2.group_ref, bf16[8,4,4,64,512]{4,3,2,1,0:T(8,128)(2,1)} %bitcast.16), custom_call_target="tpu_custom_call" | custom-call | tf_op jit(solution)/shard_map/pallas_call | solution.py:92
  7.1 0.0 copy-start
  7.1 10.0 %all-to-all-start = ((bf16[64,64,512]{2,1,0:T(8,128)(2,1)}), bf16[64,64,512]{2,1,0:T(8,128)(2,1)}, u32[]{:S(2)}, u32[]{:S(2)}) async-start(bf16[64,64,512]{2,1,0:T(8,128)(2,1)} %shard_map.68), calls=%async_computation | async-start | bytes 8388608 | tf_op jit(solution)/shard_map/all_to_all | solution.py:176
  17.1 0.0 copy-start.2
  17.2 0.0 copy-done
  17.2 4.2 %copy.8 = bf16[20000,64]{1,0:T(8,128)(2,1)} copy(bf16[20000,64]{0,1:T(8,128)(2,1)S(1)} %copy-done) | data formatting | bytes 5120000 | tf_op args[4]
  21.4 0.0 copy-done.2
  21.4 4.2 %gather_fusion = bf16[512,64]{1,0:T(8,128)(2,1)S(1)} fusion(bf16[20000,64]{1,0:T(8,128)(2,1)} %copy.8, s32[1024]{0:T(1024)S(1)} %pad_clamp_fusion), kind=kCustom, calls=%fused_computation | custom fusion | bytes 133120 | tf_op jit(solution)/shard_map/jit(_take)/gather | solution.py:177
  25.6 0.1 broadcast_select_fusion
  25.8 44.0 %all-to-all-done = bf16[64,64,512]{2,1,0:T(8,128)(2,1)} async-done(((bf16[64,64,512]{2,1,0:T(8,128)(2,1)}), bf16[64,64,512]{2,1,0:T(8,128)(2,1)}, u32[]{:S(2)}, u32[]{:S(2)}) %all-to-all-start) | async-done | bytes 4194336 | tf_op jit(solution)/shard_map/all_to_all | solution.py:176
  69.7 3.9 %shard_map.69 = (f32[128,512]{1,0:T(8,128)S(1)}, f32[128,512]{1,0:T(8,128)S(1)}, f32[128,512]{1,0:T(8,128)S(1)}, f32[128,512]{1,0:T(8,128)S(1)}) custom-call(s32[1]{0:T(128)} %bitcast.1.place_ref, bf16[4096,512]{1,0:T(8,128)(2,1)} %bitcast.7.x_hbm), custom_call_target="tpu_custom_call" | custom-call | tf_op jit(solution)/shard_map/pallas_call | solution.py:147
  73.6 9.0 %collective-permute-start = (f32[128,512]{1,0:T(8,128)S(1)}, f32[128,512]{1,0:T(8,128)S(1)}, u32[]{:S(2)}, u32[]{:S(2)}) collective-permute-start(f32[128,512]{1,0:T(8,128)S(1)} %get-tuple-element.9), channel_id=1, source_target_pairs={{1,3},{7,5},{9,11},{15,13},{8,18},{14,20},{10,24},{12,30},{11,33},... | collective-permute-start | bytes 786440 | tf_op jit(solution)/shard_map/ppermute | solution.py:183
  82.6 0.2 collective-permute-start.1
  82.9 0.8 collective-permute-start.2
  83.7 6.0 %collective-permute-start.3 = (f32[128,512]{1,0:T(8,128)S(1)}, f32[128,512]{1,0:T(8,128)S(1)}, u32[]{:S(2)}, u32[]{:S(2)}) collective-permute-start(f32[128,512]{1,0:T(8,128)S(1)} %get-tuple-element.12), channel_id=1, source_target_pairs={{1,1},{7,7},{9,9},{15,15},{8,16},{14,22},{10,26},{12,28},{11,35},{... | collective-permute-start | bytes 786440 | tf_op jit(solution)/shard_map/ppermute | solution.py:183
  90.4 0.0 collective-permute-done
  90.4 4.7 %collective-permute-done.1 = f32[128,512]{1,0:T(8,128)S(1)} collective-permute-done((f32[128,512]{1,0:T(8,128)S(1)}, f32[128,512]{1,0:T(8,128)S(1)}, u32[]{:S(2)}, u32[]{:S(2)}) %collective-permute-start.1) | collective-permute-done | bytes 262176 | tf_op jit(solution)/shard_map/ppermute | solution.py:183
  95.0 7.8 %collective-permute-done.2 = f32[128,512]{1,0:T(8,128)S(1)} collective-permute-done((f32[128,512]{1,0:T(8,128)S(1)}, f32[128,512]{1,0:T(8,128)S(1)}, u32[]{:S(2)}, u32[]{:S(2)}) %collective-permute-start.2) | collective-permute-done | bytes 262176 | tf_op jit(solution)/shard_map/ppermute | solution.py:183
  102.8 4.6 %collective-permute-done.3 = f32[128,512]{1,0:T(8,128)S(1)} collective-permute-done((f32[128,512]{1,0:T(8,128)S(1)}, f32[128,512]{1,0:T(8,128)S(1)}, u32[]{:S(2)}, u32[]{:S(2)}) %collective-permute-start.3) | collective-permute-done | bytes 262176 | tf_op jit(solution)/shard_map/ppermute | solution.py:183
  107.4 0.1 add_select_fusion
  107.5 0.0 copy-start.1
  107.5 0.9 convolution_bitcast_fusion
  108.4 0.0 copy-done.1
  (5 shorter events, 0.0 us)
Async XLA Ops:
  7.1 10.0 %copy-start = (bf16[20000,64]{0,1:T(8,128)(2,1)S(1)}, bf16[20000,64]{0,1:T(8,128)(2,1)}, u32[]{:S(2)}) copy-start(bf16[20000,64]{0,1:T(8,128)(2,1)} %param.9) | copy-start | bytes 7680004
  7.1 62.6 %all-to-all-start = ((bf16[64,64,512]{2,1,0:T(8,128)(2,1)}), bf16[64,64,512]{2,1,0:T(8,128)(2,1)}, u32[]{:S(2)}, u32[]{:S(2)}) async-start(bf16[64,64,512]{2,1,0:T(8,128)(2,1)} %shard_map.68), calls=%async_computation | async-start | bytes 8388608 | tf_op jit(solution)/shard_map/all_to_all | solution.py:176
  17.1 4.3 %copy-start.2 = (s32[1,512]{1,0:T(1,128)S(1)}, s32[1,512]{1,0:T(1,128)}, u32[]{:S(2)}) copy-start(s32[1,512]{1,0:T(1,128)} %param.8) | copy-start | bytes 6148
  73.6 16.7 %collective-permute-start = (f32[128,512]{1,0:T(8,128)S(1)}, f32[128,512]{1,0:T(8,128)S(1)}, u32[]{:S(2)}, u32[]{:S(2)}) collective-permute-start(f32[128,512]{1,0:T(8,128)S(1)} %get-tuple-element.9), channel_id=1, source_target_pairs={{1,3},{7,5},{9,11},{15,13},{8,18},{14,20},{10,24},{12,30},{11,33},... | collective-permute-start | bytes 786440 | tf_op jit(solution)/shard_map/ppermute | solution.py:183
  82.6 12.4 %collective-permute-start.1 = (f32[128,512]{1,0:T(8,128)S(1)}, f32[128,512]{1,0:T(8,128)S(1)}, u32[]{:S(2)}, u32[]{:S(2)}) collective-permute-start(f32[128,512]{1,0:T(8,128)S(1)} %get-tuple-element.10), channel_id=1, source_target_pairs={{1,0},{7,6},{9,8},{15,14},{8,17},{14,23},{10,27},{12,29},{11,34},{... | collective-permute-start | bytes 786440 | tf_op jit(solution)/shard_map/ppermute | solution.py:183
  82.9 19.9 %collective-permute-start.2 = (f32[128,512]{1,0:T(8,128)S(1)}, f32[128,512]{1,0:T(8,128)S(1)}, u32[]{:S(2)}, u32[]{:S(2)}) collective-permute-start(f32[128,512]{1,0:T(8,128)S(1)} %get-tuple-element.11), channel_id=1, source_target_pairs={{1,2},{7,4},{9,10},{15,12},{8,19},{14,21},{10,25},{12,31},{11,32},... | collective-permute-start | bytes 786440 | tf_op jit(solution)/shard_map/ppermute | solution.py:183
  83.7 23.7 %collective-permute-start.3 = (f32[128,512]{1,0:T(8,128)S(1)}, f32[128,512]{1,0:T(8,128)S(1)}, u32[]{:S(2)}, u32[]{:S(2)}) collective-permute-start(f32[128,512]{1,0:T(8,128)S(1)} %get-tuple-element.12), channel_id=1, source_target_pairs={{1,1},{7,7},{9,9},{15,15},{8,16},{14,22},{10,26},{12,28},{11,35},{... | collective-permute-start | bytes 786440 | tf_op jit(solution)/shard_map/ppermute | solution.py:183
  107.5 0.9 copy-start.1
